TPU v7x, 32 devices: a whole 2x2x4 slice. The times are simulated.
32 devices in a mesh: dp: 8 (over y, x, core), seq: 4 (over z).
Axes of the slice: x: 2, y: 2, z: 4, core: 2. Of those that a mesh axis runs over, the one named last changes fastest.
Arguments:
- tokens: bfloat16 [16, 2048, 768], P('dp', 'seq'), may hold values from -6 to 6
- segment_ids: int32 [16, 2048], P('dp', 'seq'), may hold values from 0 to 3, never falling along the last dimension, each value on 1 to 1024 neighbouring positions
- boundary_mask: int32 [16, 4, 256], P('dp'), may hold values from 0 to 1, as said below
- w_qkv: bfloat16 [768, 2304], replicated, may hold values from -0.21875 to 0.21875
- b_qkv: float32 [2304], replicated, may hold values from -3 to 3
- w_out: bfloat16 [768, 768], replicated, may hold values from -1.75 to 1.75
- b_out: float32 [768], replicated, may hold values from -3 to 3
- ln1_gain: float32 [768], replicated, may hold values from 0.1 to 1.9
- ln1_bias: float32 [768], replicated, may hold values from -3 to 3
- w_in: bfloat16 [768, 3072], replicated, may hold values from -0.21875 to 0.21875
- b_in: float32 [3072], replicated, may hold values from -3 to 3
- w_down: bfloat16 [3072, 768], replicated, may hold values from -0.109375 to 0.109375
- b_down: float32 [768], replicated, may hold values from -3 to 3
- ln2_gain: float32 [768], replicated, may hold values from 0.1 to 1.9
- ln2_bias: float32 [768], replicated, may hold values from -3 to 3
- proj_e: bfloat16 [256, 2048], P(None, 'seq'), may hold values from -0.25 to 0.25
- cotangent: bfloat16 [16, 2048, 768], P('dp', 'seq'), may hold values from -6 to 6
Outputs:
- layer_out: bfloat16 [16, 2048, 768], P('dp', 'seq')
- grad_tokens: float32 [16, 2048, 768], P('dp', 'seq')
- grad_w_qkv: float32 [768, 2304], P(('dp', 'seq'))
- grad_b_qkv: float32 [2304], P(('dp', 'seq'))
- grad_w_out: float32 [768, 768], P(('dp', 'seq'))
- grad_b_out: float32 [768], P(('dp', 'seq'))
- grad_ln1_gain: float32 [768], P(('dp', 'seq'))
- grad_ln1_bias: float32 [768], P(('dp', 'seq'))
- grad_w_in: float32 [768, 3072], P(('dp', 'seq'))
- grad_b_in: float32 [3072], P(('dp', 'seq'))
- grad_w_down: float32 [3072, 768], P(('dp', 'seq'))
- grad_b_down: float32 [768], P(('dp', 'seq'))
- grad_ln2_gain: float32 [768], P(('dp', 'seq'))
- grad_ln2_bias: float32 [768], P(('dp', 'seq'))
- grad_proj_e: float32 [256, 2048], P(None, 'seq')
Inputs may be any that keep to these rules, and one draw needn't show every extreme that they name: `segment_ids`: each sequence's ids never fall; every one of the 4 segments has 1 to 1024 positions, and one has exactly 1024. `boundary_mask`: for each sequence, each of the 256 slots is owned by exactly one of its 4 segments, and each segment owns at least one slot.
All inputs are finite; a program needn't handle non-finite values.
Results may differ from a plain program's by a relative error of at most 0.02.
Values may be sent and summed in bfloat16 or wider, within the bound.
No kernel may reach another device: no remote copies, remote signals or barrier semaphores. Data moves between devices by JAX's collectives and lax.ppermute only.
A program may use at most 192 MiB of HBM per device.

v0:
```python
import jax
import jax.numpy as jnp
from jax import lax
from jax.sharding import PartitionSpec as P

HEADS = 12
HD = 64
KP = 256
NSEG = 4
MICRO = 2


EPS = 1e-05
SCALE = 0.125
HALF_ROOT = 0.7071067811865476
INV_ROOT_TAU = 0.3989422804014327


def layer_norm(resid, gain, shift):
    center = resid - jnp.mean(resid, -1, keepdims=True)
    inverse = lax.rsqrt(jnp.mean(center * center, -1, keepdims=True) + EPS)
    normed = center * inverse
    return (normed * gain + shift, normed, inverse)


def norm_back(upstream, normed, inverse, gain):
    scaled = upstream * gain
    inner = (
        scaled
        - jnp.mean(scaled, -1, keepdims=True)
        - normed * jnp.mean(scaled * normed, -1, keepdims=True)
    )
    return (inverse * inner, jnp.sum(upstream * normed, 0), jnp.sum(upstream, 0))


def gelu_value(hidden):
    return 0.5 * hidden * (1.0 + jax.scipy.special.erf(hidden * HALF_ROOT))


def gelu_slope(hidden):
    return 0.5 * (
        1.0 + jax.scipy.special.erf(hidden * HALF_ROOT)
    ) + hidden * INV_ROOT_TAU * jnp.exp(-0.5 * hidden * hidden)


def rows_dot(left, right):
    return lax.dot_general(
        left, right, (((0,), (0,)), ((), ())), preferred_element_type=jnp.float32
    )


def back_dot(left, right):
    return lax.dot_general(
        left, right, (((1,), (1,)), ((), ())), preferred_element_type=jnp.float32
    )


def masked_scores(query, key_summary, allowed):
    scores = (
        jnp.einsum("slhd,skhd->shlk", query, key_summary, preferred_element_type=jnp.float32)
        * SCALE
    )
    return jnp.where(allowed, scores, -1e30)


def body(
    tokens,
    segment_ids,
    boundary_mask,
    w_qkv,
    b_qkv,
    w_out,
    b_out,
    ln1_gain,
    ln1_bias,
    w_in,
    b_in,
    w_down,
    b_down,
    ln2_gain,
    ln2_bias,
    proj_e,
    cotangent,
):
    seqs_dev, local_len, width = tokens.shape
    per_batch = seqs_dev // MICRO
    row_count = per_batch * local_len
    weight_list = (
        w_qkv,
        b_qkv,
        w_out,
        b_out,
        ln1_gain,
        ln1_bias,
        w_in,
        b_in,
        w_down,
        b_down,
        ln2_gain,
        ln2_bias,
    )
    totals = [jnp.zeros(w.shape, jnp.float32) for w in weight_list]
    grad_proj = jnp.zeros(proj_e.shape, jnp.float32)
    proj_rows = jnp.transpose(proj_e).astype(jnp.float32)
    out_blocks = []
    grad_blocks = []
    for batch_index in range(MICRO):
        first_seq = batch_index * per_batch
        last_seq = first_seq + per_batch
        block_tokens = tokens[first_seq:last_seq]
        segs = segment_ids[first_seq:last_seq]
        masks = boundary_mask[first_seq:last_seq].astype(jnp.float32)
        onehot = (segs[..., None] == jnp.arange(NSEG, dtype=jnp.int32)).astype(jnp.float32)
        valid = jnp.einsum("sln,snk->slk", onehot, masks)
        allowed = (valid > 0.5)[:, None]
        weighted = (proj_rows[None] * valid).astype(jnp.bfloat16)
        token_rows = block_tokens.reshape(row_count, width)
        projected = (jnp.dot(token_rows, w_qkv, preferred_element_type=jnp.float32) + b_qkv).astype(
            jnp.bfloat16
        )
        query = projected[:, :width].reshape(per_batch, local_len, HEADS, HD)
        keys_values = projected[:, width:].reshape(per_batch, local_len, 2 * width)
        partial_sums = jnp.einsum(
            "slk,slc->skc", weighted, keys_values, preferred_element_type=jnp.float32
        )
        summary = lax.psum(partial_sums.astype(jnp.bfloat16), "seq")
        key_summary = summary[..., :width].reshape(per_batch, KP, HEADS, HD)
        value_summary = summary[..., width:].reshape(per_batch, KP, HEADS, HD)
        masked = masked_scores(query, key_summary, allowed)
        top_score = jnp.max(masked, -1, keepdims=True)
        expo = jnp.exp(masked - top_score)
        total = jnp.sum(expo, -1, keepdims=True)
        probs_low = (expo / total).astype(jnp.bfloat16)
        attended = (
            jnp.einsum(
                "shlk,skhd->slhd", probs_low, value_summary, preferred_element_type=jnp.float32
            )
            .astype(jnp.bfloat16)
            .reshape(row_count, width)
        )
        first_resid = (
            token_rows.astype(jnp.float32)
            + jnp.dot(attended, w_out, preferred_element_type=jnp.float32)
            + b_out
        )
        mid, normed_one, inverse_one = layer_norm(first_resid, ln1_gain, ln1_bias)
        mid_low = mid.astype(jnp.bfloat16)
        hidden = jnp.dot(mid_low, w_in, preferred_element_type=jnp.float32) + b_in
        activ_low = gelu_value(hidden).astype(jnp.bfloat16)
        second_resid = mid + jnp.dot(activ_low, w_down, preferred_element_type=jnp.float32) + b_down
        final, normed_two, inverse_two = layer_norm(second_resid, ln2_gain, ln2_bias)
        out_blocks.append(final.astype(jnp.bfloat16).reshape(per_batch, local_len, width))
        upstream = cotangent[first_seq:last_seq].reshape(row_count, width).astype(jnp.float32)
        grad_second, grad_gain_two, grad_bias_two = norm_back(
            upstream, normed_two, inverse_two, ln2_gain
        )
        grad_branch = grad_second.astype(jnp.bfloat16)
        grad_activ = back_dot(grad_branch, w_down)
        grad_hidden = (grad_activ * gelu_slope(hidden)).astype(jnp.bfloat16)
        grad_mid = grad_second + back_dot(grad_hidden, w_in)
        grad_first, grad_gain_one, grad_bias_one = norm_back(
            grad_mid, normed_one, inverse_one, ln1_gain
        )
        grad_attn = grad_first.astype(jnp.bfloat16)
        grad_attended = (
            back_dot(grad_attn, w_out).astype(jnp.bfloat16).reshape(per_batch, local_len, HEADS, HD)
        )
        probs_again = jnp.exp(masked_scores(query, key_summary, allowed) - top_score) / total
        grad_probs = jnp.einsum(
            "slhd,skhd->shlk", grad_attended, value_summary, preferred_element_type=jnp.float32
        )
        grad_value_sum = jnp.einsum(
            "shlk,slhd->skhd",
            probs_again.astype(jnp.bfloat16),
            grad_attended,
            preferred_element_type=jnp.float32,
        )
        grad_scores = (
            probs_again
            * (grad_probs - jnp.sum(probs_again * grad_probs, -1, keepdims=True))
            * SCALE
        ).astype(jnp.bfloat16)
        grad_query = jnp.einsum(
            "shlk,skhd->slhd", grad_scores, key_summary, preferred_element_type=jnp.float32
        )
        grad_key_sum = jnp.einsum(
            "shlk,slhd->skhd", grad_scores, query, preferred_element_type=jnp.float32
        )
        local_grad = jnp.concatenate(
            [
                grad_key_sum.reshape(per_batch, KP, width),
                grad_value_sum.reshape(per_batch, KP, width),
            ],
            -1,
        )
        grad_summary = lax.psum(local_grad.astype(jnp.bfloat16), "seq")
        grad_keys_values = jnp.einsum(
            "slk,skc->slc", weighted, grad_summary, preferred_element_type=jnp.float32
        )
        grad_weighted = jnp.einsum(
            "skc,slc->slk", grad_summary, keys_values, preferred_element_type=jnp.float32
        )
        grad_proj = grad_proj + jnp.einsum("slk,slk->kl", grad_weighted, valid)
        grad_projected = jnp.concatenate(
            [grad_query.reshape(row_count, width), grad_keys_values.reshape(row_count, 2 * width)],
            -1,
        ).astype(jnp.bfloat16)
        grad_rows = grad_first + back_dot(grad_projected, w_qkv)
        grad_blocks.append(grad_rows.reshape(per_batch, local_len, width))
        terms = (
            rows_dot(token_rows, grad_projected),
            jnp.sum(grad_projected.astype(jnp.float32), 0),
            rows_dot(attended, grad_attn),
            jnp.sum(grad_attn.astype(jnp.float32), 0),
            grad_gain_one,
            grad_bias_one,
            rows_dot(mid_low, grad_hidden),
            jnp.sum(grad_hidden.astype(jnp.float32), 0),
            rows_dot(activ_low, grad_branch),
            jnp.sum(grad_branch.astype(jnp.float32), 0),
            grad_gain_two,
            grad_bias_two,
        )
        totals = [running + term for running, term in zip(totals, terms)]
    gathered = tuple(totals)
    reduced = lax.psum_scatter(gathered, ("dp", "seq"), scatter_dimension=0, tiled=True)
    grad_proj_e = lax.psum(grad_proj.astype(jnp.bfloat16), "dp").astype(jnp.float32)
    layer_out = jnp.concatenate(out_blocks, 0)
    grad_tokens = jnp.concatenate(grad_blocks, 0)
    return (
        layer_out,
        grad_tokens,
        reduced[0],
        reduced[1],
        reduced[2],
        reduced[3],
        reduced[4],
        reduced[5],
        reduced[6],
        reduced[7],
        reduced[8],
        reduced[9],
        reduced[10],
        reduced[11],
        grad_proj_e,
    )


def solution(mesh):
    placed = (
        P("dp", "seq", None),
        P("dp", "seq"),
        P("dp", None, None),
        P(),
        P(),
        P(),
        P(),
        P(),
        P(),
        P(),
        P(),
        P(),
        P(),
        P(),
        P(),
        P(None, "seq"),
        P("dp", "seq", None),
    )
    return jax.shard_map(
        body,
        mesh=mesh,
        in_specs=placed,
        out_specs=(
            P("dp", "seq", None),
            P("dp", "seq", None),
            P(("dp", "seq"), None),
            P(("dp", "seq")),
            P(("dp", "seq"), None),
            P(("dp", "seq")),
            P(("dp", "seq")),
            P(("dp", "seq")),
            P(("dp", "seq"), None),
            P(("dp", "seq")),
            P(("dp", "seq"), None),
            P(("dp", "seq")),
            P(("dp", "seq")),
            P(("dp", "seq")),
            P(None, "seq"),
        ),
        check_vma=False,
    )
```

profile of v0, /device:TPU:0, one launch (start us, length us, event | category | flops | bytes accessed | tf_op | source)
XLA Modules:
  0.0 892.7 jit_solution(5054992284339986810)
XLA Ops:
  9.2 4.7 fusion.19
  13.9 3.4 fusion.18
  22.6 3.2 fusion.43
  35.3 2.3 copy.98
  37.6 2.3 copy.93
  39.9 59.7 %all-reduce.19.cloned.1.call-done = (bf16[1,256,1536]{2,1,0:T(8,128)(2,1)}, bf16[1,256,1536]{2,1,0:T(8,128)(2,1)}) async-done(((bf16[1,256,1536]{2,1,0:T(8,128)(2,1)}, bf16[1,256,1536]{2,1,0:T(8,128)(2,1)}), (bf16[1,256,1536]{2,1,0:T(8,128)(2,1)}, bf16[1,256,1536]{2,1,0:T(8,128)(2,1)})) %all-reduce.19.cloned.1.call-update) | async-done | bytes 1572880 | tf_op jit(solution)/shard_map/psum | solution.py:126
  99.6 2.5 fusion.184
  109.8 6.9 fusion.189
  116.7 3.6 fusion.73
  122.8 6.9 fusion.187
  129.6 3.6 fusion.70
  135.0 8.4 fusion.176
  143.5 9.5 %multiply_convert_fusion.3 = (bf16[512,3072]{1,0:T(8,128)(2,1)S(1)}, bf16[512,3072]{1,0:T(8,128)(2,1)S(1)}, f32[512,3072]{1,0:T(8,128)}) fusion(f32[3072]{0:T(1024)S(1)} %copy-done.66, f32[512,3072]{1,0:T(8,128)} %fusion.176, bf16[768,3072]{1,0:T(8,128)(2,1)S(1)} %bitcast.241, f32[512,768]{1,0:T(8,128)S(1)} %get-tuple-element.120, f32[768]{0:T(1024)S(1)} %copy-done.50, ...), kind=kOutput, calls=%fused_computation.29 | convolution fusion | flops 2436759552 | bytes 25188352 | tf_op jit(solution)/shard_map/dot_general | solution.py:148
  153.1 2.8 fusion.191
  156.2 2.8 fusion.192
  162.6 2.9 convert_reduce_fusion.6
  165.6 8.2 convert_reduce_fusion
  173.7 8.1 convert_reduce_fusion.1
  181.9 3.6 multiply_reduce_fusion.3
  185.5 5.4 convert_reduce_fusion.9
  193.9 2.3 copy.101
  196.2 4.9 fusion.90
  201.2 3.6 fusion.193
  208.8 2.3 copy.106
  211.2 4.9 fusion.93
  216.0 3.6 fusion.194
  219.6 11.8 %fusion.99 = bf16[12,64,256]{2,1,0:T(8,128)(2,1)} fusion(bf16[512,12,64]{0,2,1:T(8,128)(2,1)} %bitcast.225, f32[12,512,256]{1,2,0:T(8,128)} %fusion.193, f32[12,512,256]{1,2,0:T(8,128)} %get-tuple-element.118, f32[12,512]{1,0:T(8,128)} %get-tuple-element.117), kind=kOutput, calls=%fused_computation.145 | convolution fusion | flops 212539648 | bytes 13787136 | tf_op jit(solution)/shard_map/shlk,slhd->skhd/dot_general | solution.py:186
  231.4 11.8 %fusion.96 = bf16[12,64,256]{2,1,0:T(8,128)(2,1)} fusion(bf16[512,12,64]{0,2,1:T(8,128)(2,1)} %bitcast.223, f32[12,512,256]{1,2,0:T(8,128)} %fusion.194, f32[12,512,256]{1,2,0:T(8,128)} %get-tuple-element.124, f32[12,512]{1,0:T(8,128)} %get-tuple-element.123), kind=kOutput, calls=%fused_computation.144 | convolution fusion | flops 212539648 | bytes 13787136 | tf_op jit(solution)/shard_map/shlk,slhd->skhd/dot_general | solution.py:186
  247.4 3.9 fusion.157
  251.3 64.8 %all-reduce.17.cloned.1.call-done = (bf16[256,1536]{0,1:T(8,128)(2,1)}, bf16[256,1536]{0,1:T(8,128)(2,1)}) async-done(((bf16[256,1536]{0,1:T(8,128)(2,1)}, bf16[256,1536]{0,1:T(8,128)(2,1)}), (bf16[256,1536]{0,1:T(8,128)(2,1)}, bf16[256,1536]{0,1:T(8,128)(2,1)})) %all-reduce.17.cloned.1.call-update) | async-done | bytes 1572880 | tf_op jit(solution)/shard_map/psum | solution.py:196
  316.1 2.5 fusion.108
  320.3 4.6 convolution_add_fusion.4
  325.2 11.7 %fusion.79 = bf16[12,64,512]{2,1,0:T(8,128)(2,1)} fusion(bf16[256,12,64]{0,2,1:T(8,128)(2,1)} %bitcast.229, f32[12,512,256]{1,2,0:T(8,128)} %fusion.193, f32[12,512,256]{1,2,0:T(8,128)} %get-tuple-element.118, f32[12,512]{1,0:T(8,128)} %get-tuple-element.117), kind=kOutput, calls=%fused_computation.131 | convolution fusion | flops 212736256 | bytes 13787136 | tf_op jit(solution)/shard_map/shlk,skhd->slhd/dot_general | solution.py:183
  336.9 2.3 copy.105
  339.2 11.7 %fusion.76 = bf16[12,64,512]{2,1,0:T(8,128)(2,1)} fusion(bf16[256,12,64]{0,2,1:T(8,128)(2,1)} %bitcast.231, f32[12,512,256]{1,2,0:T(8,128)} %fusion.194, f32[12,512,256]{1,2,0:T(8,128)} %get-tuple-element.124, f32[12,512]{1,0:T(8,128)} %get-tuple-element.123), kind=kOutput, calls=%fused_computation.130 | convolution fusion | flops 212736256 | bytes 13787136 | tf_op jit(solution)/shard_map/shlk,skhd->slhd/dot_general | solution.py:183
  359.7 5.1 add_bitcast_fusion
  364.8 8.0 copy.125
  373.3 5.5 fusion.178
  378.8 5.8 convolution_add_fusion.1
  384.7 5.3 fusion.160
  390.0 5.3 convolution_add_fusion
  404.2 2.8 pad_maximum_fusion.3
  408.6 41.6 %all-reduce.8 = (f32[2304]{0:T(1024)}, f32[768]{0:T(1024)}, f32[768]{0:T(1024)}, f32[768]{0:T(1024)}, f32[3072]{0:T(1024)}, /*index=5*/f32[768]{0:T(1024)}, f32[768]{0:T(1024)}, f32[768]{0:T(1024)}) all-reduce(f32[2304]{0:T(1024)} %add.266, f32[768]{0:T(1024)} %add.268, ...), channel_id=3, replica_groups=mesh['dp'=8,'seq'=4] {'dp','seq'}, use_global_device_ids=true, to_apply=%region_29.30.clone | all-reduce | flops 9984 | bytes 79872
  460.3 4.3 add_bitcast_fusion.1
  470.5 7.6 reduce-scatter.7.cloned.1.call-done
  478.0 124.2 %reduce-scatter.13.cloned.1.call-done = f32[24,2304]{1,0:T(8,128)} async-done(((f32[768,2304]{1,0:T(8,128)}), f32[24,2304]{1,0:T(8,128)}) %reduce-scatter.13.cloned.1.call-update) | async-done | bytes 221200
  602.2 142.4 %reduce-scatter.9.cloned.1.call-done = f32[24,3072]{1,0:T(8,128)} async-done(((f32[768,3072]{1,0:T(8,128)}), f32[24,3072]{1,0:T(8,128)}) %reduce-scatter.9.cloned.1.call-update) | async-done | bytes 294928 | tf_op jit(solution)/shard_map/reduce_scatter | solution.py:226
  744.6 141.0 %reduce-scatter.11.cloned.1.call-done = f32[96,768]{1,0:T(8,128)} async-done(((f32[3072,768]{1,0:T(8,128)}), f32[96,768]{1,0:T(8,128)}) %reduce-scatter.11.cloned.1.call-update) | async-done | bytes 294928 | tf_op jit(solution)/shard_map/reduce_scatter | solution.py:226
  (235 shorter events, 81.1 us)
Async XLA Ops:
  7.2 6.7 copy-start.65
  7.2 92.4 %all-reduce.19.cloned.1.call-start = ((), (), s32[]{:S(2)}) async-start(), calls=%async_computation.10 | async-start | bytes 3145728 | tf_op jit(solution)/shard_map/psum | solution.py:126
  9.2 4.7 copy-start.45
  19.1 6.6 copy-start.12
  19.1 6.6 copy-start.29
  27.3 288.8 %all-reduce.17.cloned.1.call-start = ((), (), s32[]{:S(2)}) async-start(), calls=%async_computation.9 | async-start | bytes 3145728 | tf_op jit(solution)/shard_map/psum | solution.py:196
  116.7 3.7 copy-start.46
  116.7 3.7 copy-start.62
  116.7 3.7 copy-start.67
  129.6 3.7 copy-start.47
  129.6 3.7 copy-start.63
  129.6 3.7 copy-start.68
  134.3 51.2 %copy-start.37 = (f32[512,768]{1,0:T(8,128)}, f32[512,768]{1,0:T(8,128)S(1)}, u32[]{:S(2)}) copy-start(f32[512,768]{1,0:T(8,128)S(1)} %get-tuple-element.120) | copy-start | bytes 4718596
  134.3 51.2 %copy-start.56 = (f32[512]{0:T(512)}, f32[512]{0:T(512)S(1)}, u32[]{:S(2)}) copy-start(f32[512]{0:T(512)S(1)} %broadcast_multiply_fusion.11) | copy-start | bytes 6148
  134.3 9.1 %slice-start.2 = ((s8[4718592]{0:T(1024)(128)(4,1)}), s8[4194304]{0:T(1024)(128)(4,1)S(1)}, s32[]{:S(2)}) async-start(s8[4718592]{0:T(1024)(128)(4,1)} %bitcast.240), calls=%async_computation.13 | async-start | bytes 8388608
  135.0 50.5 %copy-start.59 = (f32[512]{0:T(512)}, f32[512]{0:T(512)S(1)}, u32[]{:S(2)}) copy-start(f32[512]{0:T(512)S(1)} %add_rsqrt_fusion.3) | copy-start | bytes 6148
  135.0 8.5 slice-start.3
  135.0 8.5 copy-start.66
  135.0 18.0 %slice-start = ((s8[4718592]{0:T(1024)(128)(4,1)}), s8[4194304]{0:T(1024)(128)(4,1)S(1)}, s32[]{:S(2)}) async-start(s8[4718592]{0:T(1024)(128)(4,1)} %bitcast.238), calls=%async_computation.11 | async-start | bytes 8388608
  143.5 9.6 %slice-start.1 = ((s8[4718592]{0:T(1024)(128)(4,1)}), s8[524288]{0:T(1024)(128)(4,1)S(1)}, s32[]{:S(2)}) async-start(s8[4718592]{0:T(1024)(128)(4,1)} %bitcast.238), calls=%async_computation.12 | async-start | bytes 1048576
  143.5 9.6 %copy-start.69 = (f32[768]{0:T(1024)S(1)}, f32[768]{0:T(1024)}, u32[]{:S(2)}) copy-start(f32[768]{0:T(1024)} %param.29) | copy-start | bytes 9220
  165.6 16.3 %copy-start.16 = (f32[512,768]{1,0:T(8,128)}, f32[512,768]{1,0:T(8,128)S(1)}, u32[]{:S(2)}) copy-start(f32[512,768]{1,0:T(8,128)S(1)} %get-tuple-element.102) | copy-start | bytes 4718596
  165.6 20.0 %copy-start.14 = (f32[512,768]{1,0:T(8,128)}, f32[512,768]{1,0:T(8,128)S(1)}, u32[]{:S(2)}) copy-start(f32[512,768]{1,0:T(8,128)S(1)} %get-tuple-element.91) | copy-start | bytes 4718596
  173.7 11.8 %copy-start.22 = (bf16[512,3072]{1,0:T(8,128)(2,1)}, bf16[512,3072]{1,0:T(8,128)(2,1)S(1)}, u32[]{:S(2)}) copy-start(bf16[512,3072]{1,0:T(8,128)(2,1)S(1)} %get-tuple-element.137) | copy-start | bytes 9437188
  181.9 3.6 copy-start.70
  196.2 4.9 copy-start.24
  196.2 4.9 copy-start.36
  201.1 3.7 copy-start.61
  201.1 3.7 copy-start.60
  201.1 3.7 copy-start.3
  201.2 3.7 copy-start.40
  211.2 4.9 copy-start.25
  211.2 4.9 copy-start.35
  247.4 221.2 %all-reduce.15.cloned.1.call-start = ((), (), s32[]{:S(2)}) async-start(), calls=%async_computation.7 | async-start | bytes 524288 | tf_op jit(solution)/shard_map/psum | solution.py:227
  320.3 157.8 %reduce-scatter.7.cloned.1.call-start = ((), (), s32[]{:S(2)}) async-start(), calls=%async_computation.4 | async-start | bytes 2433024 | tf_op jit(solution)/shard_map/reduce_scatter | solution.py:226
  324.9 277.3 %reduce-scatter.13.cloned.1.call-start = ((), (), s32[]{:S(2)}) async-start(), calls=%async_computation.8 | async-start | bytes 7299072
  372.8 371.8 %reduce-scatter.9.cloned.1.call-start = ((), (), s32[]{:S(2)}) async-start(), calls=%async_computation.5 | async-start | bytes 9732096 | tf_op jit(solution)/shard_map/reduce_scatter | solution.py:226
  373.3 5.5 copy-start.4
  373.3 5.5 copy-start.23
  384.6 501.0 %reduce-scatter.11.cloned.1.call-start = ((), (), s32[]{:S(2)}) async-start(), calls=%async_computation.6 | async-start | bytes 9732096 | tf_op jit(solution)/shard_map/reduce_scatter | solution.py:226
  384.7 5.3 copy-start.11
  384.7 5.3 copy-start.15
  395.3 3.8 copy-start.51
  395.4 11.7 %copy-start.6 = (bf16[512,1536]{1,0:T(8,128)(2,1)S(1)}, bf16[512,1536]{1,0:T(8,128)(2,1)}, u32[]{:S(2)}) copy-start(bf16[512,1536]{1,0:T(8,128)(2,1)} %copy-done.5) | copy-start | bytes 4718596
  395.4 11.7 %copy-start.9 = (bf16[512,768]{1,0:T(8,128)(2,1)S(1)}, bf16[512,768]{1,0:T(8,128)(2,1)}, u32[]{:S(2)}) copy-start(bf16[512,768]{1,0:T(8,128)(2,1)} %copy.110) | copy-start | bytes 2359300
  460.3 4.3 copy-start.20
  460.3 4.3 copy-start.28
  460.3 4.3 copy-start.39
  (34 other events, 72.3 us)
Sparse Core Ops, SparseCore 0:
  27.4 72.1 all-reduce.18
  247.5 68.5 all-reduce.16
  320.4 52.5 all-reduce.14
  379.6 98.3 reduce-scatter.6
  484.1 118.0 reduce-scatter.12
  609.6 135.0 reduce-scatter.8
  751.1 134.4 reduce-scatter.10
where the time goes:
time: 898 us; the launch traced here: 893 us
  waiting for transfers between devices  540 us (60%)
  matrix products  206 us (23%)
  local copies, waits for them, and re-layouts  62.7 us (7%)
  blocking collectives  41.6 us (5%)
  other arithmetic  26.6 us (3%)
  between operations  15 us (2%)
    reduce_scatter x3, waiting for transfers between devices, body(): lax.psum_scatter(gathered, ('dp', 'seq'), scatter_dimension=0, tiled=True)  291 us
    unnamed x8, waiting for transfers between devices  124 us
    psum x1, waiting for transfers between devices, body(): grad_summary = lax.psum(local_grad.astype(jnp.bfloat16), 'seq')  64.8 us
    psum x1, waiting for transfers between devices, body(): summary = lax.psum(partial_sums.astype(jnp.bfloat16), 'seq')  59.7 us
    unnamed x1, blocking collectives  41.6 us
    dot_general x8, matrix products, rows_dot(): lax.dot_general(left, right, (((0,), (0,)), ((), ())), preferred_element_...  37.5 us
    dot_general x8, matrix products, back_dot(): lax.dot_general(left, right, (((1,), (1,)), ((), ())), preferred_element_...  35.1 us
    unnamed x161, local copies, waits for them, and re-layouts  30.9 us
  transfers between devices with their start and end apart: 7, of which 6 were waited for; matrix products, arithmetic and copies ran while one was open for 14% of the time, Pallas kernels for 0%

commit v1 on v0

v1 whole, which is shorter than its diff:
```python
import functools

import jax
import jax.numpy as jnp
from jax import lax
from jax.experimental import pallas as pl
from jax.experimental.pallas import tpu as pltpu
from jax.sharding import PartitionSpec as P

HEADS = 12
HD = 64
KP = 256
NSEG = 4
SEG_MAX = 1024
TE = 272
EPS = 1e-05
SCALE = 0.125
HALF_ROOT = 0.7071067811865476
INV_ROOT_TAU = 0.3989422804014327
F32 = jnp.float32
BF16 = jnp.bfloat16
VMEM_LIMIT = 60 * 1024 * 1024


def dot(left, right, cl=1, cr=0):
    return lax.dot_general(left, right, (((cl,), (cr,)), ((), ())), preferred_element_type=F32)


def call(kernel, out_shape, **kw):
    kw.setdefault("compiler_params", pltpu.CompilerParams(vmem_limit_bytes=VMEM_LIMIT))
    return pl.pallas_call(kernel, out_shape=out_shape, **kw)


def sds(shape, dtype=BF16):
    return jax.ShapeDtypeStruct(shape, dtype)


def cost(flops, nbytes, trans=0):
    return pl.CostEstimate(flops=int(flops), bytes_accessed=int(nbytes), transcendentals=int(trans))


def full(shape):
    return pl.BlockSpec(shape, lambda *_: (0,) * len(shape))


def prep_kernel(s, tok_ref, seg_ref, mask_ref, proj_ref, t_ref, al_ref, wt_ref):
    width = tok_ref.shape[-1]
    length = tok_ref.shape[1]
    m = mask_ref[0]
    owner = jnp.sum(m * lax.broadcasted_iota(jnp.int32, m.shape, 0), 0, keepdims=True).astype(F32)
    owner_col = jnp.transpose(jnp.broadcast_to(owner, (8, KP)))[:, 0:1]
    seg = seg_ref[s : s + 1, :].astype(F32)
    allowed = owner_col == seg
    weighted = jnp.where(allowed, proj_ref[...].astype(F32), 0.0).astype(BF16)
    al_ref[...] = jnp.where(allowed, 1.0, 0.0).astype(BF16)
    wt_ref[...] = weighted
    t_ref[0:KP, :] = dot(weighted, tok_ref[0]).astype(BF16)
    count = dot(jnp.ones((TE - KP, length), BF16), weighted, 1, 1).astype(BF16)
    t_ref[KP:TE, :] = jnp.concatenate([count, jnp.zeros((TE - KP, width - KP), BF16)], 1)


def prep(s, tokens, segment_ids, mask, proj_e):
    seqs, length, width = tokens.shape
    return call(
        functools.partial(prep_kernel, s),
        (sds((TE, width)), sds((KP, length)), sds((KP, length))),
        grid=(1,),
        in_specs=[
            pl.BlockSpec((1, length, width), lambda i: (s, 0, 0)),
            full((seqs, length)),
            pl.BlockSpec((1, NSEG, KP), lambda i: (s, 0, 0)),
            full((KP, length)),
        ],
        out_specs=(full((TE, width)), full((KP, length)), full((KP, length))),
        cost_estimate=cost(2 * KP * length * width, 2 * length * width),
        name="prep",
    )(tokens, segment_ids, mask, proj_e)


def query_kernel(me_ref, tok_ref, wq_ref, bq_ref, q_ref, tt_ref):
    units, rows = tt_ref.shape[1], tt_ref.shape[2]
    tok = tok_ref[0]
    q = (dot(tok, wq_ref[...]) + bq_ref[...]).astype(BF16).astype(F32) * SCALE
    q_ref[0] = jnp.transpose(q.astype(BF16))
    tt = jnp.transpose(tok)
    for u in range(units):
        tt_ref[0, u ^ me_ref[0]] = tt[u * rows : (u + 1) * rows]


def query(me, units, tokens, w_qkv, b_qkv):
    seqs, length, width = tokens.shape
    rows = width // units
    return call(
        query_kernel,
        (sds((seqs, width, length)), sds((seqs, units, rows, length))),
        grid_spec=pltpu.PrefetchScalarGridSpec(
            num_scalar_prefetch=1,
            grid=(seqs,),
            in_specs=[
                pl.BlockSpec((1, length, width), lambda s, me: (s, 0, 0)),
                pl.BlockSpec((width, width), lambda s, me: (0, 0)),
                pl.BlockSpec((1, width), lambda s, me: (0, 0)),
            ],
            out_specs=(
                pl.BlockSpec((1, width, length), lambda s, me: (s, 0, 0)),
                pl.BlockSpec((1, units, rows, length), lambda s, me: (s, 0, 0, 0)),
            ),
        ),
        cost_estimate=cost(2 * seqs * width * length * width, 6 * seqs * length * width),
        name="query",
    )(me, tokens, w_qkv, b_qkv)


def flip_kernel(w_ref, o_ref):
    o_ref[...] = jnp.transpose(w_ref[...])


def flip_kv(w_qkv):
    width = w_qkv.shape[0]
    return call(
        flip_kernel,
        sds((2 * width, width)),
        grid=(2,),
        in_specs=[pl.BlockSpec((width, width), lambda i: (0, 1 + i))],
        out_specs=pl.BlockSpec((width, width), lambda i: (i, 0)),
        cost_estimate=cost(0, 8 * width * width),
        name="flip_kv",
    )(w_qkv)


def norm_stats(resid):
    center = resid - jnp.mean(resid, -1, keepdims=True)
    inverse = lax.rsqrt(jnp.mean(center * center, -1, keepdims=True) + EPS)
    return center * inverse, inverse


def attend_kernel(nt, me_ref, *refs):
    t_refs = refs[:nt]
    wkv_ref, bkv_ref, q_ref, al_ref, tok_ref, wo_ref, bo_ref = refs[nt : nt + 7]
    tt_ref, c_ref, kv_ref, p_ref, att_ref, n_ref, inv_ref, att_scr = refs[nt + 7 :]
    width = wo_ref.shape[0]
    units, rows = tt_ref.shape[0], tt_ref.shape[1]
    total = t_refs[0][...].astype(F32)
    for r in t_refs[1:]:
        total = total + r[...].astype(F32)
    low = total.astype(BF16)
    t_low = low[0:KP]
    c_row = low[KP : KP + 8, 0:KP]
    c_ref[...] = c_row
    tt = jnp.transpose(t_low)
    me = me_ref[0]
    for u in range(units):
        tt_ref[u ^ me] = tt[u * rows : (u + 1) * rows]
    kv_ref[...] = (dot(wkv_ref[...], t_low, 1, 1) + bkv_ref[...] * c_row[0:1].astype(F32)).astype(BF16)
    allowed = al_ref[...] > 0.5

    def head(h, carry):
        rows_h = pl.ds(pl.multiple_of(h * HD, HD), HD)
        rows_v = pl.ds(pl.multiple_of(width + h * HD, HD), HD)
        scores = dot(kv_ref[rows_h, :], q_ref[0, rows_h, :], 0, 0)
        scores = jnp.where(allowed, scores, -1e30)
        expo = jnp.exp(scores - jnp.max(scores, 0, keepdims=True))
        probs = (expo * (1.0 / jnp.sum(expo, 0, keepdims=True))).astype(BF16)
        p_ref[h] = probs
        att_scr[rows_h, :] = dot(kv_ref[rows_v, :], probs).astype(BF16)
        return carry

    lax.fori_loop(0, width // HD, head, 0, unroll=2)
    att = att_scr[...]
    for u in range(units):
        att_ref[u ^ me] = att[u * rows : (u + 1) * rows]
    resid = tok_ref[0].astype(F32) + dot(att, wo_ref[...], 0, 0) + bo_ref[...]
    normed, inverse = norm_stats(resid)
    n_ref[...] = normed
    inv_ref[...] = inverse


def attend(me, s, units, tparts, wkv_t, bkv_col, q_t, allow, tokens, w_out, b_out):
    seqs, length, width = tokens.shape
    rows = width // units
    nt = len(tparts)
    m = lambda nd: (lambda i, me: (0,) * nd)
    return call(
        functools.partial(attend_kernel, nt),
        (
            sds((units, rows, KP)),
            sds((8, KP)),
            sds((2 * width, KP)),
            sds((width // HD, KP, length)),
            sds((units, rows, length)),
            sds((length, width), F32),
            sds((length, 1), F32),
        ),
        grid_spec=pltpu.PrefetchScalarGridSpec(
            num_scalar_prefetch=1,
            grid=(1,),
            in_specs=[pl.BlockSpec((TE, width), m(2))] * nt
            + [
                pl.BlockSpec((2 * width, width), m(2)),
                pl.BlockSpec((2 * width, 1), m(2)),
                pl.BlockSpec((1, width, length), lambda i, me: (s, 0, 0)),
                pl.BlockSpec((KP, length), m(2)),
                pl.BlockSpec((1, length, width), lambda i, me: (s, 0, 0)),
                pl.BlockSpec((width, width), m(2)),
                pl.BlockSpec((1, width), m(2)),
            ],
            out_specs=(
                pl.BlockSpec((units, rows, KP), m(3)),
                pl.BlockSpec((8, KP), m(2)),
                pl.BlockSpec((2 * width, KP), m(2)),
                pl.BlockSpec((width // HD, KP, length), m(3)),
                pl.BlockSpec((units, rows, length), m(3)),
                pl.BlockSpec((length, width), m(2)),
                pl.BlockSpec((length, 1), m(2)),
            ),
            scratch_shapes=[pltpu.VMEM((width, length), BF16)],
        ),
        cost_estimate=cost(2 * KP * width * 2 * width + 8 * KP * length * width + 2 * length * width * width, 16 * 2**20),
        name="attend",
    )(me, *tparts, wkv_t, bkv_col, q_t, allow, tokens, w_out, b_out)


def norm_back(upstream, normed, inverse, gain):
    scaled = upstream * gain
    return inverse * (
        scaled
        - jnp.mean(scaled, -1, keepdims=True)
        - normed * jnp.mean(scaled * normed, -1, keepdims=True)
    )


def feed_kernel(
    chunks, me_ref, n_ref, inv_ref, g1_ref, be1_ref, win_ref, bin_ref, wdn_ref, bdn_ref, g2_ref, be2_ref, cot_ref,
    mt_ref, at_ref, gb_ref, dh_ref, out_ref, gf_ref, gfl_ref, stat_ref, gbin_ref,
    low_scr, acc_scr, slope_scr, gb_scr,
):
    step = pl.program_id(0)
    me = me_ref[0]
    units, rows = mt_ref.shape[0], mt_ref.shape[1]
    per, arows = at_ref.shape[0], at_ref.shape[1]

    @pl.when(step == 0)
    def _():
        mid = n_ref[...] * g1_ref[...] + be1_ref[...]
        low = mid.astype(BF16)
        low_scr[...] = low
        acc_scr[...] = mid + bdn_ref[...]
        mt = jnp.transpose(low)
        for u in range(units):
            mt_ref[u ^ me] = mt[u * rows : (u + 1) * rows]

    @pl.when(step < chunks)
    def _():
        hidden = dot(low_scr[...], win_ref[...]) + bin_ref[...]
        phi = 0.5 * (1.0 + lax.erf(hidden * HALF_ROOT))
        activ = (hidden * phi).astype(BF16)
        slope_scr[step] = (phi + hidden * INV_ROOT_TAU * jnp.exp(-0.5 * hidden * hidden)).astype(BF16)
        acc_scr[...] += dot(activ, wdn_ref[...])
        at = jnp.transpose(activ)
        for i in range(per):
            at_ref[i ^ (me & (per - 1))] = at[i * arows : (i + 1) * arows]

    @pl.when(step == chunks - 1)
    def _():
        normed, inverse = norm_stats(acc_scr[...])
        out_ref[...] = (normed * g2_ref[...] + be2_ref[...]).astype(BF16)
        cot = cot_ref[0].astype(F32)
        stat_ref[0:1, :] = jnp.sum(cot * normed, 0, keepdims=True)
        stat_ref[1:2, :] = jnp.sum(cot, 0, keepdims=True)
        second = norm_back(cot, normed, inverse, g2_ref[...])
        low = second.astype(BF16)
        stat_ref[2:3, :] = jnp.sum(low.astype(F32), 0, keepdims=True)
        gb_ref[...] = low
        gb_scr[...] = low
        acc_scr[...] = second

    @pl.when(step >= chunks)
    def _():
        grad = dot(gb_scr[...], wdn_ref[...], 1, 1)
        dh = (grad * slope_scr[step - chunks].astype(F32)).astype(BF16)
        dh_ref[...] = dh
        gbin_ref[...] = jnp.sum(dh.astype(F32), 0, keepdims=True)
        acc_scr[...] += dot(dh, win_ref[...], 1, 1)

    @pl.when(step == 2 * chunks - 1)
    def _():
        up = acc_scr[...]
        normed = n_ref[...]
        stat_ref[3:4, :] = jnp.sum(up * normed, 0, keepdims=True)
        stat_ref[4:5, :] = jnp.sum(up, 0, keepdims=True)
        first = norm_back(up, normed, inv_ref[...], g1_ref[...])
        low = first.astype(BF16)
        gf_ref[...] = first
        gfl_ref[...] = low
        stat_ref[5:6, :] = jnp.sum(low.astype(F32), 0, keepdims=True)
        stat_ref[6:8, :] = jnp.zeros((2, stat_ref.shape[1]), F32)


def feed(me, s, units, normed, inverse, g1, be1, w_in, b_in, w_down, b_down, g2, be2, cot):
    length, width = normed.shape
    ff = w_in.shape[1]
    rows = width // units
    arows = ff // units
    chunk = 768
    chunks = ff // chunk
    per = chunk // arows
    fwd = lambda i: jnp.where(i < chunks, i, i - chunks)
    m = lambda nd: (lambda i, me: (0,) * nd)
    return call(
        functools.partial(feed_kernel, chunks),
        (
            sds((units, rows, length)),
            sds((units, arows, length)),
            sds((length, width)),
            sds((length, ff)),
            sds((length, width)),
            sds((length, width), F32),
            sds((length, width)),
            sds((8, width), F32),
            sds((1, ff), F32),
        ),
        grid_spec=pltpu.PrefetchScalarGridSpec(
            num_scalar_prefetch=1,
            grid=(2 * chunks,),
            in_specs=[
                pl.BlockSpec((length, width), m(2)),
                pl.BlockSpec((length, 1), m(2)),
                pl.BlockSpec((1, width), m(2)),
                pl.BlockSpec((1, width), m(2)),
                pl.BlockSpec((width, chunk), lambda i, me: (0, fwd(i))),
                pl.BlockSpec((1, chunk), lambda i, me: (0, fwd(i))),
                pl.BlockSpec((chunk, width), lambda i, me: (fwd(i), 0)),
                pl.BlockSpec((1, width), m(2)),
                pl.BlockSpec((1, width), m(2)),
                pl.BlockSpec((1, width), m(2)),
                pl.BlockSpec((1, length, width), lambda i, me: (s, 0, 0)),
            ],
            out_specs=(
                pl.BlockSpec((units, rows, length), m(3)),
                pl.BlockSpec((per, arows, length), lambda i, me: (jnp.minimum(i, chunks - 1) ^ (me[0] // per), 0, 0)),
                pl.BlockSpec((length, width), m(2)),
                pl.BlockSpec((length, chunk), lambda i, me: (0, jnp.maximum(i - chunks, 0))),
                pl.BlockSpec((length, width), m(2)),
                pl.BlockSpec((length, width), m(2)),
                pl.BlockSpec((length, width), m(2)),
                pl.BlockSpec((8, width), m(2)),
                pl.BlockSpec((1, chunk), lambda i, me: (0, jnp.maximum(i - chunks, 0))),
            ),
            scratch_shapes=[
                pltpu.VMEM((length, width), BF16),
                pltpu.VMEM((length, width), F32),
                pltpu.VMEM((chunks, length, chunk), BF16),
                pltpu.VMEM((length, width), BF16),
            ],
        ),
        cost_estimate=cost(8 * length * width * ff, 24 * 2**20, 2 * length * ff),
        name="feed",
    )(me, normed, inverse, g1, be1, w_in, b_in, w_down, b_down, g2, be2, cot)


def attend_back_kernel(gfl_ref, wo_ref, kv_ref, p_ref, q_ref, c_ref, wkv_ref, bkv_ref, dq_ref, gs_ref, gt_ref, st_ref, da_scr):
    width = wo_ref.shape[0]
    length = gfl_ref.shape[0]
    da_scr[...] = dot(wo_ref[...], gfl_ref[...], 1, 1).astype(BF16)

    def head(h, carry):
        rows_h = pl.ds(pl.multiple_of(h * HD, HD), HD)
        rows_v = pl.ds(pl.multiple_of(width + h * HD, HD), HD)
        probs = p_ref[h]
        wide = probs.astype(F32)
        da = da_scr[rows_h, :]
        grad = dot(kv_ref[rows_v, :], da, 0, 0)
        gs_ref[rows_v, :] = dot(da, probs, 1, 1).astype(BF16)
        ds = (wide * (grad - jnp.sum(wide * grad, 0, keepdims=True))).astype(BF16)
        dq_ref[rows_h, :] = (dot(kv_ref[rows_h, :], ds) * SCALE).astype(BF16)
        gs_ref[rows_h, :] = dot(q_ref[0, rows_h, :], ds, 1, 1).astype(BF16)
        return carry

    lax.fori_loop(0, width // HD, head, 0, unroll=2)
    gs = gs_ref[...]
    gt_ref[0:KP, :] = dot(gs, wkv_ref[...], 0, 0).astype(BF16)
    b_hi = bkv_ref[...].astype(BF16)
    b_lo = (bkv_ref[...] - b_hi.astype(F32)).astype(BF16)
    pad = TE - KP
    drow = dot(jnp.broadcast_to(b_hi, (pad, 2 * width)), gs) + dot(jnp.broadcast_to(b_lo, (pad, 2 * width)), gs)
    gt_ref[KP:TE, :] = jnp.concatenate([drow.astype(BF16), jnp.zeros((pad, width - KP), BF16)], 1)
    st_ref[:, 0:width] = dot(jnp.ones((8, length), BF16), dq_ref[...], 1, 1)
    st_ref[:, width:] = dot(c_ref[...], gs, 1, 1)


def attend_back(s, gfl, w_out, kv_t, probs, q_t, c_row, wkv_t, bkv_row):
    length, width = gfl.shape
    m = lambda nd: (lambda i: (0,) * nd)
    return call(
        attend_back_kernel,
        (sds((width, length)), sds((2 * width, KP)), sds((TE, width)), sds((8, 3 * width), F32)),
        grid=(1,),
        in_specs=[
            pl.BlockSpec((length, width), m(2)),
            pl.BlockSpec((width, width), m(2)),
            pl.BlockSpec((2 * width, KP), m(2)),
            pl.BlockSpec((width // HD, KP, length), m(3)),
            pl.BlockSpec((1, width, length), lambda i: (s, 0, 0)),
            pl.BlockSpec((8, KP), m(2)),
            pl.BlockSpec((2 * width, width), m(2)),
            pl.BlockSpec((1, 2 * width), m(2)),
        ],
        out_specs=(
            pl.BlockSpec((width, length), m(2)),
            pl.BlockSpec((2 * width, KP), m(2)),
            pl.BlockSpec((TE, width), m(2)),
            pl.BlockSpec((8, 3 * width), m(2)),
        ),
        scratch_shapes=[pltpu.VMEM((width, length), BF16)],
        cost_estimate=cost(2 * KP * width * 2 * width + 16 * KP * length * width + 2 * length * width * width, 12 * 2**20),
        name="attend_back",
    )(gfl, w_out, kv_t, probs, q_t, c_row, wkv_t, bkv_row)


def token_kernel(gf_ref, dq_ref, wq_ref, o_ref):
    o_ref[...] = gf_ref[...] + dot(dq_ref[...], wq_ref[...], 0, 1)


def token_grad(gf, dq_t, w_qkv):
    length, width = gf.shape
    return call(
        token_kernel,
        sds((length, width), F32),
        grid=(1,),
        in_specs=[full((length, width)), full((width, length)), pl.BlockSpec((width, width), lambda i: (0, 0))],
        out_specs=full((length, width)),
        cost_estimate=cost(2 * length * width * width, 8 * 2**20),
        name="token_grad",
    )(gf, dq_t, w_qkv)


def last_kernel(seqs, nt, *refs):
    t_refs = [refs[s * nt : (s + 1) * nt] for s in range(seqs)]
    base = seqs * nt
    part_refs = refs[base : base + seqs]
    wt_refs = refs[base + seqs : base + 2 * seqs]
    al_refs = refs[base + 2 * seqs : base + 3 * seqs]
    tok_ref = refs[base + 3 * seqs]
    o_ref, gp_ref = refs[base + 3 * seqs + 1 :]
    proj = None
    for s in range(seqs):
        total = t_refs[s][0][...].astype(F32)
        for r in t_refs[s][1:]:
            total = total + r[...].astype(F32)
        low = total[0:KP].astype(BF16)
        d_col = jnp.transpose(total[KP : KP + 8, 0:KP])[:, 0:1]
        o_ref[s] = part_refs[s][...] + dot(wt_refs[s][...], low, 0, 0)
        term = (dot(low, tok_ref[s], 1, 1) + d_col) * al_refs[s][...].astype(F32)
        proj = term if proj is None else proj + term
    gp_ref[...] = proj.astype(BF16)


def last(tparts, parts, weights, allows, tokens):
    seqs, length, width = tokens.shape
    nt = len(tparts[0])
    flat = [t for ts in tparts for t in ts]
    return call(
        functools.partial(last_kernel, seqs, nt),
        (sds((seqs, length, width), F32), sds((KP, length))),
        grid=(1,),
        in_specs=[full((TE, width))] * (seqs * nt)
        + [full((length, width))] * seqs
        + [full((KP, length))] * (2 * seqs)
        + [full((seqs, length, width))],
        out_specs=(full((seqs, length, width)), full((KP, length))),
        cost_estimate=cost(4 * seqs * length * width * KP, 12 * 2**20),
        name="last",
    )(*flat, *parts, *weights, *allows, tokens)


def down_kernel(seqs, half, order, with_recv, *refs):
    at_refs = refs[:seqs]
    gb_refs = refs[seqs : 2 * seqs]
    rest = refs[2 * seqs :]
    res = None
    for s in range(seqs):
        term = dot(at_refs[s][0, 0], gb_refs[s][...])
        res = term if res is None else res + term
    if with_recv:
        recv_ref, send_ref, keep_ref = rest
        low = (res + recv_ref[0].astype(F32)).astype(BF16)

        @pl.when(pl.program_id(0) < half)
        def _():
            send_ref[0] = low

        @pl.when(pl.program_id(0) >= half)
        def _():
            keep_ref[0] = low

    else:
        (out_ref,) = rest
        out_ref[0] = res.astype(BF16)


def down_grad(at, gb, core, recv=None, send_bit=None):
    seqs = len(at)
    units, arows, length = at[0].shape
    width = gb[0].shape[1]
    n = units // 2
    half = n // 2
    if send_bit is None:
        pick = lambda i: i
    elif send_bit == 0:
        pick = lambda i: jnp.where(i < half, 2 * i + 1, 2 * (i - half))
    else:
        pick = lambda i: (i + half) % n
    at4 = [a.reshape(n, 2, arows, length) for a in at]
    in_specs = [pl.BlockSpec((1, 1, arows, length), lambda i: (pick(i), core, 0, 0))] * seqs + [full((length, width))] * seqs
    args = [*at4, *gb]
    if recv is None:
        out_shape = sds((n, arows, width))
        out_specs = pl.BlockSpec((1, arows, width), lambda i: (i, 0, 0))
    else:
        in_specs.append(pl.BlockSpec((1, arows, width), lambda i: (pick(i), 0, 0)))
        args.append(recv)
        out_shape = (sds((half, arows, width)), sds((half, arows, width)))
        out_specs = (
            pl.BlockSpec((1, arows, width), lambda i: (jnp.minimum(i, half - 1), 0, 0)),
            pl.BlockSpec((1, arows, width), lambda i: (jnp.maximum(i - half, 0), 0, 0)),
        )
    return call(
        functools.partial(down_kernel, seqs, half, None, recv is not None),
        out_shape,
        grid=(n,),
        in_specs=in_specs,
        out_specs=out_specs,
        cost_estimate=cost(2 * seqs * n * arows * length * width, 10 * 2**20),
        name="down_grad",
    )(*args)


def split_store(low, send_ref, keep_ref, send_bit, where):
    n = low.shape[0]
    if send_bit == 0:
        for i in range(n):
            (send_ref if i & 1 else keep_ref)[i // 2, :, where] = low[i]
    else:
        half = n // 2
        keep_ref[:, :, where] = low[:half]
        send_ref[:, :, where] = low[half:]


def in_kernel(seqs, send_bit, *refs):
    mt_refs = refs[:seqs]
    dh_refs = refs[seqs : 2 * seqs]
    rest = refs[2 * seqs :]
    n, _, rows, length = mt_refs[0].shape
    res = None
    for s in range(seqs):
        term = dot(mt_refs[s][...].reshape(n * rows, length), dh_refs[s][...])
        res = term if res is None else res + term
    res = res.reshape(n, rows, res.shape[-1])
    if send_bit is None:
        rest[0][...] = res.astype(BF16)
    else:
        recv_ref, send_ref, keep_ref = rest
        low = (res + recv_ref[...].astype(F32)).astype(BF16)
        split_store(low, send_ref, keep_ref, send_bit, slice(None))


def in_grad(mt, dh, core, recv=None, send_bit=None):
    seqs = len(mt)
    units, rows, length = mt[0].shape
    ff = dh[0].shape[1]
    n = units // 2
    chunk = 768
    mt4 = [a.reshape(n, 2, rows, length) for a in mt]
    in_specs = [pl.BlockSpec((n, 1, rows, length), lambda i: (0, core, 0, 0))] * seqs + [
        pl.BlockSpec((length, chunk), lambda i: (0, i))
    ] * seqs
    args = [*mt4, *dh]
    if recv is None:
        out_shape = sds((n, rows, ff))
        out_specs = pl.BlockSpec((n, rows, chunk), lambda i: (0, 0, i))
    else:
        in_specs.append(pl.BlockSpec((n, rows, chunk), lambda i: (0, 0, i)))
        args.append(recv)
        out_shape = (sds((n // 2, rows, ff)), sds((n // 2, rows, ff)))
        out_specs = (pl.BlockSpec((n // 2, rows, chunk), lambda i: (0, 0, i)),) * 2
    return call(
        functools.partial(in_kernel, seqs, send_bit),
        out_shape,
        grid=(ff // chunk,),
        in_specs=in_specs,
        out_specs=out_specs,
        cost_estimate=cost(2 * seqs * n * rows * length * ff, 10 * 2**20),
        name="in_grad",
    )(*args)


def rest_kernel(seqs, core, send_bit, me_ref, *refs):
    at_refs, gf_refs, tk_refs, dq_refs, tt_refs, gs_refs = [refs[k * seqs : (k + 1) * seqs] for k in range(6)]
    st_ref = refs[6 * seqs]
    rest = refs[6 * seqs + 1 :]
    n, _, rows, _ = at_refs[0].shape
    width = gf_refs[0].shape[1]

    def put(res, where):
        res = res.reshape(n, rows, res.shape[-1])
        if send_bit is None:
            rest[0][:, :, where] = res.astype(BF16)
        else:
            recv_ref, send_ref, keep_ref = rest
            low = (res + recv_ref[:, :, where].astype(F32)).astype(BF16)
            split_store(low, send_ref, keep_ref, send_bit, where)

    def flat(ref):
        return ref[...].reshape(n * rows, ref.shape[-1])

    def total(terms):
        out = terms[0]
        for t in terms[1:]:
            out = out + t
        return out

    put(total([dot(flat(a), g[...]) for a, g in zip(at_refs, gf_refs)]), slice(0, width))
    put(total([dot(flat(a), g[...], 1, 1) for a, g in zip(tk_refs, dq_refs)]), slice(width, 2 * width))
    put(total([dot(flat(a), g[...], 1, 1) for a, g in zip(tt_refs, gs_refs)]), slice(2 * width, 4 * width))
    stats = jnp.stack([st_ref[(2 * i + core) ^ me_ref[0]] for i in range(n)])
    put(stats.astype(F32).reshape(n * rows, 128), slice(4 * width, 4 * width + 128))


def rest_grad(me, att, gfl, tok_t, dq_t, t_t, gs_t, stats, core, recv=None, send_bit=None):
    seqs = len(att)
    units, rows, length = att[0].shape
    width = gfl[0].shape[1]
    n = units // 2
    cols = 4 * width + 128
    m = lambda nd: (lambda i, me: (0,) * nd)
    half = lambda last: pl.BlockSpec((n, 1, rows, last), lambda i, me: (0, core, 0, 0))
    cut = lambda a: a.reshape(n, 2, rows, a.shape[-1])
    in_specs = (
        [half(length)] * seqs
        + [pl.BlockSpec((length, width), m(2))] * seqs
        + [half(length)] * seqs
        + [pl.BlockSpec((width, length), m(2))] * seqs
        + [half(KP)] * seqs
        + [pl.BlockSpec((2 * width, KP), m(2))] * seqs
        + [pl.BlockSpec((units, rows, 128), m(3))]
    )
    args = [*map(cut, att), *gfl, *map(cut, tok_t), *dq_t, *map(cut, t_t), *gs_t, stats]
    if recv is None:
        out_shape = sds((n, rows, cols))
        out_specs = pl.BlockSpec((n, rows, cols), m(3))
    else:
        in_specs.append(pl.BlockSpec((n, rows, cols), m(3)))
        args.append(recv)
        out_shape = (sds((n // 2, rows, cols)),) * 2
        out_specs = (pl.BlockSpec((n // 2, rows, cols), m(3)),) * 2
    return call(
        functools.partial(rest_kernel, seqs, core, send_bit),
        out_shape,
        grid_spec=pltpu.PrefetchScalarGridSpec(num_scalar_prefetch=1, grid=(1,), in_specs=in_specs, out_specs=out_specs),
        cost_estimate=cost(seqs * n * rows * (4 * length * width + 4 * KP * width), 12 * 2**20),
        name="rest_grad",
    )(me, *args)


def add(a, b):
    return (a.astype(F32) + b.astype(F32)).astype(BF16)


def body(n_dp, n_seq, tokens, segment_ids, mask, w_qkv, b_qkv, w_out, b_out, ln1_gain, ln1_bias, w_in, b_in, w_down, b_down, ln2_gain, ln2_bias, proj_e, cotangent):
    seqs, length, width = tokens.shape
    ff = w_in.shape[1]
    n_all = n_dp * n_seq
    fast = n_dp == 8 and n_seq == 4 and length % 128 == 0
    units = 8
    dp = lax.axis_index("dp").astype(jnp.int32)
    sq = lax.axis_index("seq").astype(jnp.int32)
    me = (dp if fast else jnp.zeros((), jnp.int32)).reshape(1)
    row = lambda v: v.reshape(1, -1)

    def swap(x, bit):
        pairs = [(i, i ^ bit) for i in range(n_all)]
        return lax.ppermute(x, ("dp", "seq"), pairs)

    def along(own):
        if not fast:
            return [lax.psum(own, "seq")]
        right = [(i, i + 1) for i in range(n_seq - 1)]
        left = [(i + 1, i) for i in range(n_seq - 1)]
        out, up, down = [own], own, own
        for _ in range(min(n_seq - 1, -(-(SEG_MAX - 1) // length))):
            up = lax.ppermute(up, "seq", right)
            down = lax.ppermute(down, "seq", left)
            out += [up, down]
        return out

    prepped = [prep(s, tokens, segment_ids, mask, proj_e) for s in range(seqs)]
    tparts = [along(p[0]) for p in prepped]
    q_t, tok_t = query(me, units, tokens, w_qkv, row(b_qkv))
    wkv_t = flip_kv(w_qkv)
    bkv = b_qkv[width:]

    tt, crow, kv, probs, att, normed, inverse = [], [], [], [], [], [], []
    mt, at, gb, dh, outs, gf, gfl, stat, gbin = [], [], [], [], [], [], [], [], []
    for s in range(seqs):
        res = attend(me, s, units, tparts[s], wkv_t, bkv.reshape(-1, 1), q_t, prepped[s][1], tokens, w_out, row(b_out))
        for store, value in zip((tt, crow, kv, probs, att, normed, inverse), res):
            store.append(value)
        res = feed(me, s, units, normed[s], inverse[s], row(ln1_gain), row(ln1_bias), w_in, row(b_in), w_down, row(b_down), row(ln2_gain), row(ln2_bias), cotangent)
        for store, value in zip((mt, at, gb, dh, outs, gf, gfl, stat, gbin), res):
            store.append(value)

    X_BIT, Y_BIT, CORE = 2 * n_seq, 4 * n_seq, n_seq

    def finish(recv, keep, bit, rows_u):
        send = add(keep[1], recv[1])
        keep = add(keep[0], recv[0])
        recv = swap(send, bit)
        cols = keep.shape[-1]
        shape = (2, 2, rows_u // 4, cols)
        z0, z1 = sq & 1, sq >> 1
        pick = lambda a, z: lax.dynamic_index_in_dim(a, z, 1, keepdims=False)
        keep, recv = keep.reshape(shape), recv.reshape(shape)
        send = add(pick(keep, 1 - z0), pick(recv, 1 - z0))
        keep = add(pick(keep, z0), pick(recv, z0))
        recv = swap(send, 1)
        pick = lambda a, z: lax.dynamic_index_in_dim(a, z, 0, keepdims=False)
        send = add(pick(keep, 1 - z1), pick(recv, 1 - z1))
        keep = add(pick(keep, z1), pick(recv, z1))
        recv = swap(send, 2)
        return keep.astype(F32) + recv.astype(F32)

    if fast:
        send1 = down_grad(at, gb, 1)
        recv1 = swap(send1, CORE)
        send2 = in_grad(mt, dh, 1)
        recv2 = swap(send2, CORE)
        sx1, kx1 = down_grad(at, gb, 0, recv1, 0)
        rx1 = swap(sx1, X_BIT)
        sx2, kx2 = in_grad(mt, dh, 0, recv2, 1)
        rx2 = swap(sx2, Y_BIT)

    back = [attend_back(s, gfl[s], w_out, kv[s], probs[s], q_t, crow[s], wkv_t, row(bkv)) for s in range(seqs)]
    gparts = [along(b[2]) for b in back]
    dq_t = [b[0] for b in back]
    gs_t = [b[1] for b in back]

    st = functools.reduce(jnp.add, stat)
    st_in = functools.reduce(jnp.add, gbin)[0]
    st_qkv = functools.reduce(jnp.add, [b[3][0] for b in back])
    tok_u = [tok_t[s] for s in range(seqs)]
    if fast:
        vectors = [st_qkv, st[5], st[3], st[4], st_in, st[2], st[0], st[1]]
        flat = jnp.concatenate([v.reshape(n_all, -1) for v in vectors], 1)
        used = flat.shape[1]
        flat = jnp.pad(flat, ((0, 0), (0, 384 - used))).reshape(n_all, 3, 128)
        rows_u = width // n_dp
        flat = jnp.pad(flat, ((0, 0), (0, width // n_all - 3), (0, 0))).reshape(units, rows_u, 128).astype(BF16)
        send3 = rest_grad(me, att, gfl, tok_u, dq_t, tt, gs_t, flat, 1)
        recv3 = swap(send3, CORE)
        sx3, kx3 = rest_grad(me, att, gfl, tok_u, dq_t, tt, gs_t, flat, 0, recv3, 0)
        rx3 = swap(sx3, X_BIT)

    parts = [token_grad(gf[s], dq_t[s], w_qkv) for s in range(seqs)]
    grad_tokens, gproj = last(gparts, parts, [p[2] for p in prepped], [p[1] for p in prepped], tokens)
    layer_out = jnp.stack(outs)

    if not fast:
        join = lambda v: v.reshape(-1, v.shape[-1])
        pair = lambda a: functools.reduce(jnp.add, [dot(join(l), r) for l, r in a])
        zeros = jnp.zeros((units, width // units, 128), BF16)
        both = [rest_grad(me, att, gfl, tok_u, dq_t, tt, gs_t, zeros, c) for c in (0, 1)]
        g3 = jnp.stack(both, 1).reshape(width, -1)
        g2 = jnp.stack([in_grad(mt, dh, c) for c in (0, 1)], 1).reshape(width, -1)
        g1 = jnp.stack([down_grad(at, gb, c) for c in (0, 1)], 1).reshape(ff, width)
        grads = (g3[:, width : 4 * width], st_qkv, g3[:, :width], st[5], st[3], st[4], g2, st_in, g1, st[2], st[0], st[1])
        grads = lax.psum_scatter(tuple(g.astype(F32) for g in grads), ("dp", "seq"), scatter_dimension=0, tiled=True)
        gproj = lax.psum(gproj, "dp").astype(F32)
        return (layer_out, grad_tokens, *grads, gproj)

    g1 = finish(rx1, kx1, Y_BIT, ff // n_dp)
    g2 = finish(rx2, kx2, X_BIT, width // n_dp)
    g3 = finish(rx3, kx3, Y_BIT, width // n_dp)
    for bit in (CORE, X_BIT, Y_BIT):
        gproj = add(gproj, swap(gproj, bit))
    small = g3[:3, 4 * width :].reshape(-1)
    sizes = [v.shape[0] // n_all for v in vectors]
    cuts, at_ = [], 0
    for size in sizes:
        cuts.append(small[at_ : at_ + size])
        at_ += size
    gb_qkv, gb_out, g_g1, g_b1, gb_in, gb_down, g_g2, g_b2 = cuts
    return (
        layer_out, grad_tokens, g3[:, width : 4 * width], gb_qkv, g3[:, :width], gb_out, g_g1, g_b1,
        g2, gb_in, g1, gb_down, g_g2, g_b2, gproj.astype(F32),
    )


def solution(mesh):
    both = ("dp", "seq")
    placed = (
        P("dp", "seq", None),
        P("dp", "seq"),
        P("dp", None, None),
        *([P()] * 12),
        P(None, "seq"),
        P("dp", "seq", None),
    )
    out = (
        P("dp", "seq", None),
        P("dp", "seq", None),
        P(both, None),
        P(both),
        P(both, None),
        P(both),
        P(both),
        P(both),
        P(both, None),
        P(both),
        P(both, None),
        P(both),
        P(both),
        P(both),
        P(None, "seq"),
    )
    run = functools.partial(body, mesh.shape["dp"], mesh.shape["seq"])
    return jax.shard_map(run, mesh=mesh, in_specs=placed, out_specs=out, check_vma=False)
```

time: 898 us -> 338 us (0.38)
  waiting for transfers between devices: 540 us -> 69.5 us
  matrix products: 206 us -> 0 us
  Pallas kernels: 0 us -> 164 us
  starting transfers between devices: 1.2 us -> 71 us
  local copies, waits for them, and re-layouts: 62.7 us -> 16.7 us
  blocking collectives: 41.6 us -> 0 us
  other arithmetic: 26.6 us -> 11.5 us
  between operations: 15 us -> 1.61 us
    reduce_scatter x3 -> x0, waiting for transfers between devices: 291 us -> none  [body(): lax.psum_scatter(gathered, ('dp', 'seq'), scatter_dimension=0, tiled=True)]
    dot_general x42 -> x0, matrix products: 192 us -> none  [the longest x8 37.5 us: rows_dot(): lax.dot_general(left, right, (((0,), (0,)), ((), ())), preferred_element_...]
    pallas_call x0 -> x19, Pallas kernels: none -> 164 us  [the longest x2 45.2 us: feed(): call(functools.partial(feed_kernel, chunks), (sds((units, rows, length)),...]
    psum x3 -> x0, waiting for transfers between devices: 124 us -> none  [the longest x1 64.8 us: body(): grad_summary = lax.psum(local_grad.astype(jnp.bfloat16), 'seq')]
    unnamed x8 -> x0, waiting for transfers between devices: 124 us -> none
    ppermute x0 -> x34, starting transfers between devices: none -> 71 us  [the longest x8 38.5 us: along(): up = lax.ppermute(up, 'seq', right)]
    ppermute x0 -> x34, waiting for transfers between devices: none -> 69.5 us  [the longest x18 54.4 us: swap(): return lax.ppermute(x, ('dp', 'seq'), pairs)]
    unnamed x1 -> x0, blocking collectives: 41.6 us -> none
  transfers between devices with their start and end apart: 7 -> 34, of which waited for: 6 -> 12; matrix products, arithmetic and copies ran while one was open for 14% -> 7% of each run, Pallas kernels for 0% -> 48%
where the time goes in v1:
time: 338 us; the launch traced here: 334 us
  Pallas kernels  164 us (49%)
  starting transfers between devices  71 us (21%)
  waiting for transfers between devices  69.5 us (21%)
  local copies, waits for them, and re-layouts  16.7 us (5%)
  other arithmetic  11.5 us (3%)
    ppermute x18, waiting for transfers between devices, swap(): return lax.ppermute(x, ('dp', 'seq'), pairs)  54.4 us
    pallas_call x2, Pallas kernels, feed(): call(functools.partial(feed_kernel, chunks), (sds((units, rows, length)),...  45.2 us
    ppermute x8, starting transfers between devices, along(): up = lax.ppermute(up, 'seq', right)  38.5 us
    pallas_call x2, Pallas kernels, attend_back(): call(attend_back_kernel, (sds((width, length)), sds((2 * width, KP)), sds...  25.5 us
    pallas_call x2, Pallas kernels, attend(): call(functools.partial(attend_kernel, nt), (sds((units, rows, KP)), sds((...  25.5 us
    ppermute x18, starting transfers between devices, swap(): return lax.ppermute(x, ('dp', 'seq'), pairs)  22 us
    ppermute x8, waiting for transfers between devices, along(): down = lax.ppermute(down, 'seq', left)  14.7 us
    pallas_call x2, Pallas kernels, rest_grad(): call(functools.partial(rest_kernel, seqs, core, send_bit), out_shape, gri...  13.7 us
  transfers between devices with their start and end apart: 34, of which 12 were waited for; matrix products, arithmetic and copies ran while one was open for 7% of the time, Pallas kernels for 48%

profile of v1, /device:TPU:0, one launch (start us, length us, event | category | flops | bytes accessed | tf_op | source)
XLA Modules:
  0.0 334.1 jit_solution(8346682111583372667)
XLA Ops:
  0.6 2.6 prep.3
  3.3 5.1 %collective-permute-start.4 = (bf16[272,768]{1,0:T(8,128)(2,1)}, bf16[272,768]{1,0:T(8,128)(2,1)S(1)}, u32[]{:S(2)}, u32[]{:S(2)}) collective-permute-start(bf16[272,768]{1,0:T(8,128)(2,1)} %get-tuple-element.77.refs_0_), channel_id=1, source_target_pairs={{0,1},{1,2},{2,3},{4,5},{5,6},{6,7},{8,9},{9,10},{10,11},{12,13},{... | collective-permute-start | bytes 1253384 | tf_op jit(solution)/shard_map/ppermute | solution.py:691
  9.6 2.6 prep.2
  12.2 4.6 %collective-permute-start = (bf16[272,768]{1,0:T(8,128)(2,1)}, bf16[272,768]{1,0:T(8,128)(2,1)S(1)}, u32[]{:S(2)}, u32[]{:S(2)}) collective-permute-start(bf16[272,768]{1,0:T(8,128)(2,1)} %get-tuple-element.71.refs_0_), channel_id=1, source_target_pairs={{0,1},{1,2},{2,3},{4,5},{5,6},{6,7},{8,9},{9,10},{10,11},{12,13},{... | collective-permute-start | bytes 1253384 | tf_op jit(solution)/shard_map/ppermute | solution.py:691
  18.5 4.3 %collective-permute-start.6 = (bf16[272,768]{1,0:T(8,128)(2,1)S(1)}, bf16[272,768]{1,0:T(8,128)(2,1)S(1)}, u32[]{:S(2)}, u32[]{:S(2)}) collective-permute-start(bf16[272,768]{1,0:T(8,128)(2,1)S(1)} %collective-permute-done.4.refs_1_), channel_id=1, source_target_pairs={{0,1},{1,2},{2,3},{4,5},{5,6},{6,7},{8,9},{9,10},{10,11},{12,13},{... | collective-permute-start | bytes 1253384 | tf_op jit(solution)/shard_map/ppermute | solution.py:691
  26.5 3.1 flip_kv.1.refs_5_.wkv_ref
  33.2 4.4 %query.1 = (bf16[2,768,512]{2,1,0:T(8,128)(2,1)}, bf16[2,8,96,512]{3,2,1,0:T(8,128)(2,1)}) custom-call(s32[1]{0:T(128)} %bitcast.me_ref, bf16[2,512,768]{2,1,0:T(8,128)(2,1)} %refs_16_.1, bf16[768,2304]{1,0:T(8,128)(2,1)} %wq_ref.5, f32[1,2304]{1,0:T(1,128)} %reshape.234.bq_ref), custom_call_target="tpu_custom_call" | custom-call | flops 1207959552 | bytes 4718592 | tf_op jit(solution)/shard_map/query/pallas_call | solution.py:93
  37.6 2.8 fusion.19
  40.4 4.6 %collective-permute-start.2 = (bf16[272,768]{1,0:T(8,128)(2,1)S(1)}, bf16[272,768]{1,0:T(8,128)(2,1)S(1)}, u32[]{:S(2)}, u32[]{:S(2)}) collective-permute-start(bf16[272,768]{1,0:T(8,128)(2,1)S(1)} %collective-permute-done.refs_1_), channel_id=1, source_target_pairs={{0,1},{1,2},{2,3},{4,5},{5,6},{6,7},{8,9},{9,10},{10,11},{12,13},{... | collective-permute-start | bytes 1253384 | tf_op jit(solution)/shard_map/ppermute | solution.py:691
  47.4 12.7 %attend.3 = (bf16[8,96,256]{2,1,0:T(8,128)(2,1)}, bf16[8,256]{1,0:T(8,128)(2,1)}, bf16[1536,256]{1,0:T(8,128)(2,1)}, bf16[12,256,512]{2,1,0:T(8,128)(2,1)}, bf16...) custom-call(s32[1]{0:T(128)} %bitcast.me_ref, bf16[272,768]{1,0:T(8,128)(2,1)} %get-tuple-element.77.refs_0_, ...), custom_call_target="tpu_custom_call" | custom-call | flops 2013265920 | bytes 16777216 | tf_op jit(solution)/shard_map/attend/pallas_call | solution.py:183
  60.1 22.7 %feed.3 = (bf16[8,96,512]{2,1,0:T(8,128)(2,1)}, bf16[8,384,512]{2,1,0:T(8,128)(2,1)}, bf16[512,768]{1,0:T(8,128)(2,1)}, bf16[512,3072]{1,0:T(8,128)(2,1)}, bf16[...) custom-call(s32[1]{0:T(128)} %bitcast.me_ref, ...), custom_call_target="tpu_custom_call" | custom-call | flops 9663676416 | bytes 25165824 | tf_op jit(solution)/shard_map/feed/pallas_call | solution.py:309
  82.7 12.6 %attend_back.3 = (bf16[768,512]{1,0:T(8,128)(2,1)}, bf16[1536,256]{1,0:T(8,128)(2,1)}, bf16[272,768]{1,0:T(8,128)(2,1)}, f32[8,2304]{1,0:T(8,128)}) custom-call(bf16[512,768]{1,0:T(8,128)(2,1)} %get-tuple-element.87.gfl_ref.refs_3_, bf16[768,768]{1,0:T(8,128)(2,1)} %wo_ref.3, bf16[1536,256]{1,0:T(8,128)(2,1)} %get-tuple-element.88.kv_ref, ...), custom_call_target="tpu_custom_call" | custom-call | flops 2818572288 | bytes 12582912 | tf_op jit(solution)/shard_map/attend_back/pallas_call | solution.py:394
  95.3 4.8 %collective-permute-start.12 = (bf16[272,768]{1,0:T(8,128)(2,1)}, bf16[272,768]{1,0:T(8,128)(2,1)S(1)}, u32[]{:S(2)}, u32[]{:S(2)}) collective-permute-start(bf16[272,768]{1,0:T(8,128)(2,1)} %get-tuple-element.91.refs_5_), channel_id=1, source_target_pairs={{0,1},{1,2},{2,3},{4,5},{5,6},{6,7},{8,9},{9,10},{10,11},{12,13},{... | collective-permute-start | bytes 1253384 | tf_op jit(solution)/shard_map/ppermute | solution.py:691
  101.0 12.8 %attend.2 = (bf16[8,96,256]{2,1,0:T(8,128)(2,1)}, bf16[8,256]{1,0:T(8,128)(2,1)}, bf16[1536,256]{1,0:T(8,128)(2,1)}, bf16[12,256,512]{2,1,0:T(8,128)(2,1)}, bf16...) custom-call(s32[1]{0:T(128)} %bitcast.me_ref, bf16[272,768]{1,0:T(8,128)(2,1)} %get-tuple-element.71.refs_0_, ...), custom_call_target="tpu_custom_call" | custom-call | flops 2013265920 | bytes 16777216 | tf_op jit(solution)/shard_map/attend/pallas_call | solution.py:183
  113.8 22.6 %feed.2 = (bf16[8,96,512]{2,1,0:T(8,128)(2,1)}, bf16[8,384,512]{2,1,0:T(8,128)(2,1)}, bf16[512,768]{1,0:T(8,128)(2,1)}, bf16[512,3072]{1,0:T(8,128)(2,1)}, bf16[...) custom-call(s32[1]{0:T(128)} %bitcast.me_ref, ...), custom_call_target="tpu_custom_call" | custom-call | flops 9663676416 | bytes 25165824 | tf_op jit(solution)/shard_map/feed/pallas_call | solution.py:309
  136.4 6.3 %down_grad.2 = bf16[4,384,768]{2,1,0:T(8,128)(2,1)} custom-call(bf16[4,2,384,512]{3,2,1,0:T(8,128)(2,1)} %bitcast.76, bf16[4,2,384,512]{3,2,1,0:T(8,128)(2,1)} %bitcast.74, bf16[512,768]{1,0:T(8,128)(2,1)} %get-tuple-element.122.refs_2_, bf16[512,768]{1,0:T(8,128)(2,1)} %get-tuple-element.123.refs_3_), custom_call_target="tpu_custom_call" | custom-call | flops 2415919104 | bytes 10485760 | tf_op jit(solution)/shard_map/down_grad/pallas_call | solution.py:527
  142.6 6.5 %in_grad.2 = bf16[4,96,3072]{2,1,0:T(8,128)(2,1)} custom-call(bf16[4,2,96,512]{3,2,1,0:T(8,128)(2,1)} %bitcast.88, bf16[4,2,96,512]{3,2,1,0:T(8,128)(2,1)} %bitcast.86, bf16[512,3072]{1,0:T(8,128)(2,1)} %get-tuple-element.116.refs_2_, bf16[512,3072]{1,0:T(8,128)(2,1)} %get-tuple-element.117.refs_3_), custom_call_target="tpu_custom_call" | custom-call | flops 2415919104 | bytes 10485760 | tf_op jit(solution)/shard_map/in_grad/pallas_call | solution.py:586
  149.7 12.9 %attend_back.2 = (bf16[768,512]{1,0:T(8,128)(2,1)}, bf16[1536,256]{1,0:T(8,128)(2,1)}, bf16[272,768]{1,0:T(8,128)(2,1)}, f32[8,2304]{1,0:T(8,128)}) custom-call(bf16[512,768]{1,0:T(8,128)(2,1)} %get-tuple-element.82.gfl_ref.refs_2_, bf16[768,768]{1,0:T(8,128)(2,1)} %wo_ref.3, bf16[1536,256]{1,0:T(8,128)(2,1)} %get-tuple-element.83.kv_ref, ...), custom_call_target="tpu_custom_call" | custom-call | flops 2818572288 | bytes 12582912 | tf_op jit(solution)/shard_map/attend_back/pallas_call | solution.py:394
  165.3 6.4 %rest_grad.2 = bf16[4,96,3200]{2,1,0:T(8,128)(2,1)} custom-call(s32[1]{0:T(128)} %bitcast.me_ref, bf16[4,2,96,512]{3,2,1,0:T(8,128)(2,1)} %bitcast.84, bf16[4,2,96,512]{3,2,1,0:T(8,128)(2,1)} %bitcast.82, bf16[512,768]{1,0:T(8,128)(2,1)} %get-tuple-element.82.gfl_ref.refs_2_, bf16[512,768]{1,0:T(8,128)(2,1)} %get-tuple-element.87.gfl_ref.refs_3_, ...), custom_call_target="tpu_custom_call" | custom-call | flops 1811939328 | bytes 12582912 | tf_op jit(solution)/shard_map/rest_grad/pallas_call | solution.py:656
  173.1 5.3 %collective-permute-start.8 = (bf16[272,768]{1,0:T(8,128)(2,1)S(1)}, bf16[272,768]{1,0:T(8,128)(2,1)}, u32[]{:S(2)}, u32[]{:S(2)}) collective-permute-start(bf16[272,768]{1,0:T(8,128)(2,1)S(1)} %copy-done.6), channel_id=1, source_target_pairs={{0,1},{1,2},{2,3},{4,5},{5,6},{6,7},{8,9},{9,10},{10,11},{12,13},{... | collective-permute-start | bytes 1253384 | tf_op jit(solution)/shard_map/ppermute | solution.py:691
  178.4 7.4 %collective-permute-done.13.refs_7_ = bf16[272,768]{1,0:T(8,128)(2,1)} collective-permute-done((bf16[272,768]{1,0:T(8,128)(2,1)S(1)}, bf16[272,768]{1,0:T(8,128)(2,1)}, u32[]{:S(2)}, u32[]{:S(2)}) %collective-permute-start.13) | collective-permute-done | bytes 417824 | tf_op jit(solution)/shard_map/ppermute | solution.py:692
  187.1 4.6 %collective-permute-start.14 = (bf16[272,768]{1,0:T(8,128)(2,1)S(1)}, bf16[272,768]{1,0:T(8,128)(2,1)S(1)}, u32[]{:S(2)}, u32[]{:S(2)}) collective-permute-start(bf16[272,768]{1,0:T(8,128)(2,1)S(1)} %collective-permute-done.12.refs_6_), channel_id=1, source_target_pairs={{0,1},{1,2},{2,3},{4,5},{5,6},{6,7},{8,9},{9,10},{10,11},{12,13},{... | collective-permute-start | bytes 1253384 | tf_op jit(solution)/shard_map/ppermute | solution.py:691
  191.7 7.3 %collective-permute-done.9.refs_2_ = bf16[272,768]{1,0:T(8,128)(2,1)S(1)} collective-permute-done((bf16[272,768]{1,0:T(8,128)(2,1)S(1)}, bf16[272,768]{1,0:T(8,128)(2,1)S(1)}, u32[]{:S(2)}, u32[]{:S(2)}) %collective-permute-start.9) | collective-permute-done | bytes 417824 | tf_op jit(solution)/shard_map/ppermute | solution.py:692
  200.3 5.3 %collective-permute-start.10 = (bf16[272,768]{1,0:T(8,128)(2,1)}, bf16[272,768]{1,0:T(8,128)(2,1)}, u32[]{:S(2)}, u32[]{:S(2)}) collective-permute-start(bf16[272,768]{1,0:T(8,128)(2,1)} %collective-permute-done.8.refs_1_), channel_id=1, source_target_pairs={{0,1},{1,2},{2,3},{4,5},{5,6},{6,7},{8,9},{9,10},{10,11},{12,13},{... | collective-permute-start | bytes 1253384 | tf_op jit(solution)/shard_map/ppermute | solution.py:691
  206.9 3.9 %token_grad.3.refs_11_ = f32[512,768]{1,0:T(8,128)} custom-call(f32[512,768]{1,0:T(8,128)} %get-tuple-element.94.gf_ref, bf16[768,512]{1,0:T(8,128)(2,1)} %get-tuple-element.95.dq_ref.refs_7_, bf16[768,2304]{1,0:T(8,128)(2,1)} %wq_ref.5), custom_call_target="tpu_custom_call" | custom-call | flops 603979776 | bytes 8388608 | tf_op jit(solution)/shard_map/token_grad/pallas_call | solution.py:426
  210.8 3.9 %token_grad.2.refs_10_ = f32[512,768]{1,0:T(8,128)} custom-call(f32[512,768]{1,0:T(8,128)} %get-tuple-element.92.gf_ref, bf16[768,512]{1,0:T(8,128)(2,1)} %get-tuple-element.93.dq_ref.refs_6_, bf16[768,2304]{1,0:T(8,128)(2,1)} %wq_ref.5), custom_call_target="tpu_custom_call" | custom-call | flops 603979776 | bytes 8388608 | tf_op jit(solution)/shard_map/token_grad/pallas_call | solution.py:426
  214.8 7.1 %down_grad.3 = (bf16[2,384,768]{2,1,0:T(8,128)(2,1)}, bf16[2,384,768]{2,1,0:T(8,128)(2,1)}) custom-call(bf16[4,2,384,512]{3,2,1,0:T(8,128)(2,1)} %bitcast.77, bf16[4,2,384,512]{3,2,1,0:T(8,128)(2,1)} %bitcast.75, bf16[512,768]{1,0:T(8,128)(2,1)} %get-tuple-element.122.refs_2_, bf16[512,768]{1,0:T(8,128)(2,1)} %get-tuple-element.123.refs_3_, ...), custom_call_target="tpu_custom_call" | custom-call | flops 2415919104 | bytes 10485760 | tf_op jit(solution)/shard_map/down_grad/pallas_call | solution.py:527
  221.8 1.5 collective-permute-start.27
  223.4 6.6 %last.1 = (f32[2,512,768]{2,1,0:T(8,128)}, bf16[256,512]{1,0:T(8,128)(2,1)}) custom-call(bf16[272,768]{1,0:T(8,128)(2,1)} %get-tuple-element.86.refs_0_, bf16[272,768]{1,0:T(8,128)(2,1)} %collective-permute-done.8.refs_1_, bf16[272,768]{1,0:T(8,128)(2,1)} %copy-done.12, bf16[272,768]{1,0:T(8,128)(2,1)} %collective-permute-done.10.refs_3_, ...), custom_call_target="tpu_custom_call" | custom-call | flops 805306368 | bytes 12582912 | tf_op jit(solution)/shard_map/last/pallas_call | solution.py:462
  230.1 6.9 %in_grad.3 = (bf16[2,96,3072]{2,1,0:T(8,128)(2,1)}, bf16[2,96,3072]{2,1,0:T(8,128)(2,1)}) custom-call(bf16[4,2,96,512]{3,2,1,0:T(8,128)(2,1)} %bitcast.89, bf16[4,2,96,512]{3,2,1,0:T(8,128)(2,1)} %bitcast.87, bf16[512,3072]{1,0:T(8,128)(2,1)} %get-tuple-element.116.refs_2_, bf16[512,3072]{1,0:T(8,128)(2,1)} %get-tuple-element.117.refs_3_, ...), custom_call_target="tpu_custom_call" | custom-call | flops 2415919104 | bytes 10485760 | tf_op jit(solution)/shard_map/in_grad/pallas_call | solution.py:586
  237.0 1.7 collective-permute-start.22
  240.5 2.4 pad_maximum_fusion
  244.3 7.2 %rest_grad.3 = (bf16[2,96,3200]{2,1,0:T(8,128)(2,1)}, bf16[2,96,3200]{2,1,0:T(8,128)(2,1)}) custom-call(s32[1]{0:T(128)} %bitcast.me_ref, bf16[4,2,96,512]{3,2,1,0:T(8,128)(2,1)} %bitcast.85, bf16[4,2,96,512]{3,2,1,0:T(8,128)(2,1)} %bitcast.83, bf16[512,768]{1,0:T(8,128)(2,1)} %get-tuple-element.82.gfl_ref.refs_2_, ...), custom_call_target="tpu_custom_call" | custom-call | flops 1811939328 | bytes 12582912 | tf_op jit(solution)/shard_map/rest_grad/pallas_call | solution.py:656
  253.9 2.3 collective-permute-start.33
  256.3 2.0 add_convert_fusion.3
  258.3 7.8 %collective-permute-done.22 = bf16[2,96,3072]{2,1,0:T(8,128)(2,1)} collective-permute-done((bf16[2,96,3072]{2,1,0:T(8,128)(2,1)}, bf16[2,96,3072]{2,1,0:T(8,128)(2,1)}, u32[]{:S(2)}, u32[]{:S(2)}) %collective-permute-start.22) | collective-permute-done | bytes 1179680 | tf_op jit(solution)/shard_map/ppermute | solution.py:682
  266.2 1.7 add_convert_fusion.5
  268.6 13.1 %collective-permute-done.17 = bf16[2,96,3200]{2,1,0:T(8,128)(2,1)S(1)} collective-permute-done((bf16[2,96,3200]{2,1,0:T(8,128)(2,1)}, bf16[2,96,3200]{2,1,0:T(8,128)(2,1)S(1)}, u32[]{:S(2)}, u32[]{:S(2)}) %collective-permute-start.17) | collective-permute-done | bytes 1228832 | tf_op jit(solution)/shard_map/ppermute | solution.py:682
  282.8 10.5 %collective-permute-done.23 = bf16[96,3072]{1,0:T(8,128)(2,1)S(1)} collective-permute-done((bf16[96,3072]{1,0:T(8,128)(2,1)S(1)}, bf16[96,3072]{1,0:T(8,128)(2,1)S(1)}, u32[]{:S(2)}, u32[]{:S(2)}) %collective-permute-start.23) | collective-permute-done | bytes 589856 | tf_op jit(solution)/shard_map/ppermute | solution.py:682
  293.4 2.7 collective-permute-start.24
  297.2 6.8 %collective-permute-done.24 = bf16[2,24,3072]{2,1,0:T(8,128)(2,1)S(1)} collective-permute-done((bf16[2,24,3072]{2,1,0:T(8,128)(2,1)S(1)}, bf16[2,24,3072]{2,1,0:T(8,128)(2,1)S(1)}, u32[]{:S(2)}, u32[]{:S(2)}) %collective-permute-start.24) | collective-permute-done | bytes 294944 | tf_op jit(solution)/shard_map/ppermute | solution.py:682
  304.1 2.8 collective-permute-start.25
  307.1 3.7 %collective-permute-start.19 = (bf16[2,24,3200]{2,1,0:T(8,128)(2,1)S(1)}, bf16[2,24,3200]{2,1,0:T(8,128)(2,1)S(1)}, u32[]{:S(2)}, u32[]{:S(2)}) collective-permute-start(bf16[2,24,3200]{2,1,0:T(8,128)(2,1)S(1)} %get-tuple-element.142), channel_id=1, source_target_pairs={{0,1},{1,0},{2,3},{3,2},{4,5},{5,4},{6,7},{7,6},{8,9},{9,8},{10,11... | collective-permute-start | bytes 921608 | tf_op jit(solution)/shard_map/ppermute | solution.py:682
  310.7 4.3 %collective-permute-done.29 = bf16[2,96,768]{2,1,0:T(8,128)(2,1)S(1)} collective-permute-done((bf16[2,96,768]{2,1,0:T(8,128)(2,1)S(1)}, bf16[2,96,768]{2,1,0:T(8,128)(2,1)S(1)}, u32[]{:S(2)}, u32[]{:S(2)}) %collective-permute-start.29) | collective-permute-done | bytes 294944 | tf_op jit(solution)/shard_map/ppermute | solution.py:682
  316.4 4.1 %collective-permute-done.19 = bf16[2,24,3200]{2,1,0:T(8,128)(2,1)S(1)} collective-permute-done((bf16[2,24,3200]{2,1,0:T(8,128)(2,1)S(1)}, bf16[2,24,3200]{2,1,0:T(8,128)(2,1)S(1)}, u32[]{:S(2)}, u32[]{:S(2)}) %collective-permute-start.19) | collective-permute-done | bytes 307232 | tf_op jit(solution)/shard_map/ppermute | solution.py:682
  320.5 2.4 collective-permute-start.20
  322.8 4.7 %collective-permute-done.30 = bf16[96,768]{1,0:T(8,128)(2,1)S(1)} collective-permute-done((bf16[96,768]{1,0:T(8,128)(2,1)S(1)}, bf16[96,768]{1,0:T(8,128)(2,1)S(1)}, u32[]{:S(2)}, u32[]{:S(2)}) %collective-permute-start.30) | collective-permute-done | bytes 147488 | tf_op jit(solution)/shard_map/ppermute | solution.py:682
  328.4 2.2 collective-permute-done.20
  (148 shorter events, 36.0 us)
Async XLA Ops:
  3.3 20.9 %copy-start.19 = (f32[2304]{0:T(1024)S(1)}, f32[2304]{0:T(1024)}, u32[]{:S(2)}) copy-start(f32[2304]{0:T(1024)} %param.21) | copy-start | bytes 27652
  3.3 15.2 %collective-permute-start.4 = (bf16[272,768]{1,0:T(8,128)(2,1)}, bf16[272,768]{1,0:T(8,128)(2,1)S(1)}, u32[]{:S(2)}, u32[]{:S(2)}) collective-permute-start(bf16[272,768]{1,0:T(8,128)(2,1)} %get-tuple-element.77.refs_0_), channel_id=1, source_target_pairs={{0,1},{1,2},{2,3},{4,5},{5,6},{6,7},{8,9},{9,10},{10,11},{12,13},{... | collective-permute-start | bytes 1253384 | tf_op jit(solution)/shard_map/ppermute | solution.py:691
  8.3 14.5 %collective-permute-start.5 = (bf16[272,768]{1,0:T(8,128)(2,1)}, bf16[272,768]{1,0:T(8,128)(2,1)S(1)}, u32[]{:S(2)}, u32[]{:S(2)}) collective-permute-start(bf16[272,768]{1,0:T(8,128)(2,1)} %get-tuple-element.77.refs_0_), channel_id=1, source_target_pairs={{1,0},{2,1},{3,2},{5,4},{6,5},{7,6},{9,8},{10,9},{11,10},{13,12},{... | collective-permute-start | bytes 1253384 | tf_op jit(solution)/shard_map/ppermute | solution.py:692
  12.2 28.2 %collective-permute-start = (bf16[272,768]{1,0:T(8,128)(2,1)}, bf16[272,768]{1,0:T(8,128)(2,1)S(1)}, u32[]{:S(2)}, u32[]{:S(2)}) collective-permute-start(bf16[272,768]{1,0:T(8,128)(2,1)} %get-tuple-element.71.refs_0_), channel_id=1, source_target_pairs={{0,1},{1,2},{2,3},{4,5},{5,6},{6,7},{8,9},{9,10},{10,11},{12,13},{... | collective-permute-start | bytes 1253384 | tf_op jit(solution)/shard_map/ppermute | solution.py:691
  16.8 28.2 %collective-permute-start.1 = (bf16[272,768]{1,0:T(8,128)(2,1)}, bf16[272,768]{1,0:T(8,128)(2,1)S(1)}, u32[]{:S(2)}, u32[]{:S(2)}) collective-permute-start(bf16[272,768]{1,0:T(8,128)(2,1)} %get-tuple-element.71.refs_0_), channel_id=1, source_target_pairs={{1,0},{2,1},{3,2},{5,4},{6,5},{7,6},{9,8},{10,9},{11,10},{13,12},{... | collective-permute-start | bytes 1253384 | tf_op jit(solution)/shard_map/ppermute | solution.py:692
  18.5 11.1 %copy-start.9 = (bf16[272,768]{1,0:T(8,128)(2,1)}, bf16[272,768]{1,0:T(8,128)(2,1)S(1)}, u32[]{:S(2)}) copy-start(bf16[272,768]{1,0:T(8,128)(2,1)S(1)} %collective-permute-done.4.refs_1_) | copy-start | bytes 1253380
  18.5 28.0 %collective-permute-start.6 = (bf16[272,768]{1,0:T(8,128)(2,1)S(1)}, bf16[272,768]{1,0:T(8,128)(2,1)S(1)}, u32[]{:S(2)}, u32[]{:S(2)}) collective-permute-start(bf16[272,768]{1,0:T(8,128)(2,1)S(1)} %collective-permute-done.4.refs_1_), channel_id=1, source_target_pairs={{0,1},{1,2},{2,3},{4,5},{5,6},{6,7},{8,9},{9,10},{10,11},{12,13},{... | collective-permute-start | bytes 1253384 | tf_op jit(solution)/shard_map/ppermute | solution.py:691
  22.8 23.7 %collective-permute-start.7 = (bf16[272,768]{1,0:T(8,128)(2,1)S(1)}, bf16[272,768]{1,0:T(8,128)(2,1)S(1)}, u32[]{:S(2)}, u32[]{:S(2)}) collective-permute-start(bf16[272,768]{1,0:T(8,128)(2,1)S(1)} %collective-permute-done.5.refs_2_), channel_id=1, source_target_pairs={{1,0},{2,1},{3,2},{5,4},{6,5},{7,6},{9,8},{10,9},{11,10},{13,12},{... | collective-permute-start | bytes 1253384 | tf_op jit(solution)/shard_map/ppermute | solution.py:692
  40.4 19.6 %copy-start.7 = (bf16[272,768]{1,0:T(8,128)(2,1)}, bf16[272,768]{1,0:T(8,128)(2,1)S(1)}, u32[]{:S(2)}) copy-start(bf16[272,768]{1,0:T(8,128)(2,1)S(1)} %collective-permute-done.refs_1_) | copy-start | bytes 1253380
  40.4 59.7 %collective-permute-start.2 = (bf16[272,768]{1,0:T(8,128)(2,1)S(1)}, bf16[272,768]{1,0:T(8,128)(2,1)S(1)}, u32[]{:S(2)}, u32[]{:S(2)}) collective-permute-start(bf16[272,768]{1,0:T(8,128)(2,1)S(1)} %collective-permute-done.refs_1_), channel_id=1, source_target_pairs={{0,1},{1,2},{2,3},{4,5},{5,6},{6,7},{8,9},{9,10},{10,11},{12,13},{... | collective-permute-start | bytes 1253384 | tf_op jit(solution)/shard_map/ppermute | solution.py:691
  45.0 15.1 %copy-start.8 = (bf16[272,768]{1,0:T(8,128)(2,1)}, bf16[272,768]{1,0:T(8,128)(2,1)S(1)}, u32[]{:S(2)}) copy-start(bf16[272,768]{1,0:T(8,128)(2,1)S(1)} %collective-permute-done.1.refs_2_) | copy-start | bytes 1253380
  45.0 55.1 %collective-permute-start.3 = (bf16[272,768]{1,0:T(8,128)(2,1)S(1)}, bf16[272,768]{1,0:T(8,128)(2,1)S(1)}, u32[]{:S(2)}, u32[]{:S(2)}) collective-permute-start(bf16[272,768]{1,0:T(8,128)(2,1)S(1)} %collective-permute-done.1.refs_2_), channel_id=1, source_target_pairs={{1,0},{2,1},{3,2},{5,4},{6,5},{7,6},{9,8},{10,9},{11,10},{13,12},{... | collective-permute-start | bytes 1253384 | tf_op jit(solution)/shard_map/ppermute | solution.py:692
  95.3 77.7 %collective-permute-start.12 = (bf16[272,768]{1,0:T(8,128)(2,1)}, bf16[272,768]{1,0:T(8,128)(2,1)S(1)}, u32[]{:S(2)}, u32[]{:S(2)}) collective-permute-start(bf16[272,768]{1,0:T(8,128)(2,1)} %get-tuple-element.91.refs_5_), channel_id=1, source_target_pairs={{0,1},{1,2},{2,3},{4,5},{5,6},{6,7},{8,9},{9,10},{10,11},{12,13},{... | collective-permute-start | bytes 1253384 | tf_op jit(solution)/shard_map/ppermute | solution.py:691
  142.6 62.9 %collective-permute-start.26 = (bf16[4,384,768]{2,1,0:T(8,128)(2,1)}, bf16[4,384,768]{2,1,0:T(8,128)(2,1)}, u32[]{:S(2)}, u32[]{:S(2)}) collective-permute-start(bf16[4,384,768]{2,1,0:T(8,128)(2,1)} %down_grad.2), channel_id=1, source_target_pairs={{0,4},{1,5},{2,6},{3,7},{4,0},{5,1},{6,2},{7,3},{8,12},{9,13},{10,... | collective-permute-start | bytes 7077896 | tf_op jit(solution)/shard_map/ppermute | solution.py:682
  149.2 80.9 %collective-permute-start.21 = (bf16[4,96,3072]{2,1,0:T(8,128)(2,1)}, bf16[4,96,3072]{2,1,0:T(8,128)(2,1)}, u32[]{:S(2)}, u32[]{:S(2)}) collective-permute-start(bf16[4,96,3072]{2,1,0:T(8,128)(2,1)} %in_grad.2), channel_id=1, source_target_pairs={{0,4},{1,5},{2,6},{3,7},{4,0},{5,1},{6,2},{7,3},{8,12},{9,13},{10,... | collective-permute-start | bytes 7077896 | tf_op jit(solution)/shard_map/ppermute | solution.py:682
  149.7 14.0 %copy-start.20 = (f32[8,768]{1,0:T(8,128)S(1)}, f32[8,768]{1,0:T(8,128)}, u32[]{:S(2)}) copy-start(f32[8,768]{1,0:T(8,128)} %get-tuple-element.109) | copy-start | bytes 73732
  149.7 14.0 %copy-start.21 = (f32[8,768]{1,0:T(8,128)S(1)}, f32[8,768]{1,0:T(8,128)}, u32[]{:S(2)}) copy-start(f32[8,768]{1,0:T(8,128)} %get-tuple-element.108) | copy-start | bytes 73732
  149.7 14.6 %copy-start.22 = (f32[1,3072]{1,0:T(1,128)S(1)}, f32[1,3072]{1,0:T(1,128)}, u32[]{:S(2)}) copy-start(f32[1,3072]{1,0:T(1,128)} %get-tuple-element.111) | copy-start | bytes 36868
  149.7 14.6 %copy-start.23 = (f32[1,3072]{1,0:T(1,128)S(1)}, f32[1,3072]{1,0:T(1,128)}, u32[]{:S(2)}) copy-start(f32[1,3072]{1,0:T(1,128)} %get-tuple-element.110) | copy-start | bytes 36868
  165.3 7.8 %copy-start.6 = (bf16[272,768]{1,0:T(8,128)(2,1)S(1)}, bf16[272,768]{1,0:T(8,128)(2,1)}, u32[]{:S(2)}) copy-start(bf16[272,768]{1,0:T(8,128)(2,1)} %get-tuple-element.86.refs_0_) | copy-start | bytes 1253380
  171.8 71.1 %collective-permute-start.16 = (bf16[4,96,3200]{2,1,0:T(8,128)(2,1)}, bf16[4,96,3200]{2,1,0:T(8,128)(2,1)S(1)}, u32[]{:S(2)}, u32[]{:S(2)}) collective-permute-start(bf16[4,96,3200]{2,1,0:T(8,128)(2,1)} %rest_grad.2), channel_id=1, source_target_pairs={{0,4},{1,5},{2,6},{3,7},{4,0},{5,1},{6,2},{7,3},{8,12},{9,13},{10,... | collective-permute-start | bytes 7372808 | tf_op jit(solution)/shard_map/ppermute | solution.py:682
  171.8 14.0 %collective-permute-start.13 = (bf16[272,768]{1,0:T(8,128)(2,1)S(1)}, bf16[272,768]{1,0:T(8,128)(2,1)}, u32[]{:S(2)}, u32[]{:S(2)}) collective-permute-start(bf16[272,768]{1,0:T(8,128)(2,1)S(1)} %copy-done.4), channel_id=1, source_target_pairs={{1,0},{2,1},{3,2},{5,4},{6,5},{7,6},{9,8},{10,9},{11,10},{13,12},{... | collective-permute-start | bytes 1253384 | tf_op jit(solution)/shard_map/ppermute | solution.py:692
  173.1 37.7 %copy-start.5 = (bf16[272,768]{1,0:T(8,128)(2,1)}, bf16[272,768]{1,0:T(8,128)(2,1)S(1)}, u32[]{:S(2)}) copy-start(bf16[272,768]{1,0:T(8,128)(2,1)S(1)} %collective-permute-done.12.refs_6_) | copy-start | bytes 1253380
  173.1 14.0 %collective-permute-start.8 = (bf16[272,768]{1,0:T(8,128)(2,1)S(1)}, bf16[272,768]{1,0:T(8,128)(2,1)}, u32[]{:S(2)}, u32[]{:S(2)}) collective-permute-start(bf16[272,768]{1,0:T(8,128)(2,1)S(1)} %copy-done.6), channel_id=1, source_target_pairs={{0,1},{1,2},{2,3},{4,5},{5,6},{6,7},{8,9},{9,10},{10,11},{12,13},{... | collective-permute-start | bytes 1253384 | tf_op jit(solution)/shard_map/ppermute | solution.py:691
  185.8 13.1 %collective-permute-start.9 = (bf16[272,768]{1,0:T(8,128)(2,1)S(1)}, bf16[272,768]{1,0:T(8,128)(2,1)S(1)}, u32[]{:S(2)}, u32[]{:S(2)}) collective-permute-start(bf16[272,768]{1,0:T(8,128)(2,1)S(1)} %copy-done.6), channel_id=1, source_target_pairs={{1,0},{2,1},{3,2},{5,4},{6,5},{7,6},{9,8},{10,9},{11,10},{13,12},{... | collective-permute-start | bytes 1253384 | tf_op jit(solution)/shard_map/ppermute | solution.py:692
  187.1 13.1 %collective-permute-start.14 = (bf16[272,768]{1,0:T(8,128)(2,1)S(1)}, bf16[272,768]{1,0:T(8,128)(2,1)S(1)}, u32[]{:S(2)}, u32[]{:S(2)}) collective-permute-start(bf16[272,768]{1,0:T(8,128)(2,1)S(1)} %collective-permute-done.12.refs_6_), channel_id=1, source_target_pairs={{0,1},{1,2},{2,3},{4,5},{5,6},{6,7},{8,9},{9,10},{10,11},{12,13},{... | collective-permute-start | bytes 1253384 | tf_op jit(solution)/shard_map/ppermute | solution.py:691
  198.9 11.9 %copy-start.12 = (bf16[272,768]{1,0:T(8,128)(2,1)}, bf16[272,768]{1,0:T(8,128)(2,1)S(1)}, u32[]{:S(2)}) copy-start(bf16[272,768]{1,0:T(8,128)(2,1)S(1)} %collective-permute-done.9.refs_2_) | copy-start | bytes 1253380
  198.9 22.9 %collective-permute-start.15 = (bf16[272,768]{1,0:T(8,128)(2,1)}, bf16[272,768]{1,0:T(8,128)(2,1)S(1)}, u32[]{:S(2)}, u32[]{:S(2)}) collective-permute-start(bf16[272,768]{1,0:T(8,128)(2,1)} %collective-permute-done.13.refs_7_), channel_id=1, source_target_pairs={{1,0},{2,1},{3,2},{5,4},{6,5},{7,6},{9,8},{10,9},{11,10},{13,12},{... | collective-permute-start | bytes 1253384 | tf_op jit(solution)/shard_map/ppermute | solution.py:692
  200.3 23.1 %collective-permute-start.10 = (bf16[272,768]{1,0:T(8,128)(2,1)}, bf16[272,768]{1,0:T(8,128)(2,1)}, u32[]{:S(2)}, u32[]{:S(2)}) collective-permute-start(bf16[272,768]{1,0:T(8,128)(2,1)} %collective-permute-done.8.refs_1_), channel_id=1, source_target_pairs={{0,1},{1,2},{2,3},{4,5},{5,6},{6,7},{8,9},{9,10},{10,11},{12,13},{... | collective-permute-start | bytes 1253384 | tf_op jit(solution)/shard_map/ppermute | solution.py:691
  205.6 17.8 %collective-permute-start.11 = (bf16[272,768]{1,0:T(8,128)(2,1)S(1)}, bf16[272,768]{1,0:T(8,128)(2,1)}, u32[]{:S(2)}, u32[]{:S(2)}) collective-permute-start(bf16[272,768]{1,0:T(8,128)(2,1)S(1)} %collective-permute-done.9.refs_2_), channel_id=1, source_target_pairs={{1,0},{2,1},{3,2},{5,4},{6,5},{7,6},{9,8},{10,9},{11,10},{13,12},{... | collective-permute-start | bytes 1253384 | tf_op jit(solution)/shard_map/ppermute | solution.py:692
  221.8 34.4 %collective-permute-start.27 = (bf16[2,384,768]{2,1,0:T(8,128)(2,1)}, bf16[2,384,768]{2,1,0:T(8,128)(2,1)}, u32[]{:S(2)}, u32[]{:S(2)}) collective-permute-start(bf16[2,384,768]{2,1,0:T(8,128)(2,1)} %get-tuple-element.125), channel_id=1, source_target_pairs={{0,8},{1,9},{2,10},{3,11},{4,12},{5,13},{6,14},{7,15},{8,0},{9,1},... | collective-permute-start | bytes 3538952 | tf_op jit(solution)/shard_map/ppermute | solution.py:682
  230.0 8.7 %copy-start.18 = (bf16[256,512]{1,0:T(8,128)(2,1)S(1)}, bf16[256,512]{1,0:T(8,128)(2,1)}, u32[]{:S(2)}) copy-start(bf16[256,512]{1,0:T(8,128)(2,1)} %get-tuple-element.126) | copy-start | bytes 786436
  230.0 8.7 %collective-permute-start.31 = (bf16[256,512]{1,0:T(8,128)(2,1)}, bf16[256,512]{1,0:T(8,128)(2,1)}, u32[]{:S(2)}, u32[]{:S(2)}) collective-permute-start(bf16[256,512]{1,0:T(8,128)(2,1)} %get-tuple-element.126), channel_id=1, source_target_pairs={{0,4},{1,5},{2,6},{3,7},{4,0},{5,1},{6,2},{7,3},{8,12},{9,13},{10,... | collective-permute-start | bytes 786440 | tf_op jit(solution)/shard_map/ppermute | solution.py:682
  237.0 29.1 %collective-permute-start.22 = (bf16[2,96,3072]{2,1,0:T(8,128)(2,1)}, bf16[2,96,3072]{2,1,0:T(8,128)(2,1)}, u32[]{:S(2)}, u32[]{:S(2)}) collective-permute-start(bf16[2,96,3072]{2,1,0:T(8,128)(2,1)} %get-tuple-element.119), channel_id=1, source_target_pairs={{0,16},{1,17},{2,18},{3,19},{4,20},{5,21},{6,22},{7,23},{8,24},{9,... | collective-permute-start | bytes 3538952 | tf_op jit(solution)/shard_map/ppermute | solution.py:682
  239.7 14.1 %collective-permute-start.32 = (bf16[256,512]{1,0:T(8,128)(2,1)S(1)}, bf16[256,512]{1,0:T(8,128)(2,1)S(1)}, u32[]{:S(2)}, u32[]{:S(2)}) collective-permute-start(bf16[256,512]{1,0:T(8,128)(2,1)S(1)} %add_convert_fusion.14), channel_id=1, source_target_pairs={{0,8},{1,9},{2,10},{3,11},{4,12},{5,13},{6,14},{7,15},{8,0},{9,1},... | collective-permute-start | bytes 786440 | tf_op jit(solution)/shard_map/ppermute | solution.py:682
  251.6 30.1 %collective-permute-start.17 = (bf16[2,96,3200]{2,1,0:T(8,128)(2,1)}, bf16[2,96,3200]{2,1,0:T(8,128)(2,1)S(1)}, u32[]{:S(2)}, u32[]{:S(2)}) collective-permute-start(bf16[2,96,3200]{2,1,0:T(8,128)(2,1)} %get-tuple-element.113), channel_id=1, source_target_pairs={{0,8},{1,9},{2,10},{3,11},{4,12},{5,13},{6,14},{7,15},{8,0},{9,1},... | collective-permute-start | bytes 3686408 | tf_op jit(solution)/shard_map/ppermute | solution.py:682
  253.9 42.2 %collective-permute-start.33 = (bf16[256,512]{1,0:T(8,128)(2,1)S(1)}, bf16[256,512]{1,0:T(8,128)(2,1)S(1)}, u32[]{:S(2)}, u32[]{:S(2)}) collective-permute-start(bf16[256,512]{1,0:T(8,128)(2,1)S(1)} %add_convert_fusion.13), channel_id=1, source_target_pairs={{0,16},{1,17},{2,18},{3,19},{4,20},{5,21},{6,22},{7,23},{8,24},{9,... | collective-permute-start | bytes 786440 | tf_op jit(solution)/shard_map/ppermute | solution.py:682
  256.3 9.9 %copy-start.2 = (bf16[2,96,3072]{2,1,0:T(8,128)(2,1)S(1)}, bf16[2,96,3072]{2,1,0:T(8,128)(2,1)}, u32[]{:S(2)}) copy-start(bf16[2,96,3072]{2,1,0:T(8,128)(2,1)} %get-tuple-element.118) | copy-start | bytes 3538948
  258.2 38.8 %collective-permute-start.28 = (bf16[384,768]{1,0:T(8,128)(2,1)S(1)}, bf16[384,768]{1,0:T(8,128)(2,1)S(1)}, u32[]{:S(2)}, u32[]{:S(2)}) collective-permute-start(bf16[384,768]{1,0:T(8,128)(2,1)S(1)} %get-tuple-element.136), channel_id=1, source_target_pairs={{0,16},{1,17},{2,18},{3,19},{4,20},{5,21},{6,22},{7,23},{8,24},{9,... | collective-permute-start | bytes 1769480 | tf_op jit(solution)/shard_map/ppermute | solution.py:682
  266.2 15.5 %copy-start.1 = (bf16[2,96,3200]{2,1,0:T(8,128)(2,1)S(1)}, bf16[2,96,3200]{2,1,0:T(8,128)(2,1)}, u32[]{:S(2)}) copy-start(bf16[2,96,3200]{2,1,0:T(8,128)(2,1)} %get-tuple-element.112) | copy-start | bytes 3686404
  267.9 25.4 %collective-permute-start.23 = (bf16[96,3072]{1,0:T(8,128)(2,1)S(1)}, bf16[96,3072]{1,0:T(8,128)(2,1)S(1)}, u32[]{:S(2)}, u32[]{:S(2)}) collective-permute-start(bf16[96,3072]{1,0:T(8,128)(2,1)S(1)} %get-tuple-element.138), channel_id=1, source_target_pairs={{0,8},{1,9},{2,10},{3,11},{4,12},{5,13},{6,14},{7,15},{8,0},{9,1},... | collective-permute-start | bytes 1769480 | tf_op jit(solution)/shard_map/ppermute | solution.py:682
  282.0 24.9 %collective-permute-start.18 = (bf16[96,3200]{1,0:T(8,128)(2,1)S(1)}, bf16[96,3200]{1,0:T(8,128)(2,1)S(1)}, u32[]{:S(2)}, u32[]{:S(2)}) collective-permute-start(bf16[96,3200]{1,0:T(8,128)(2,1)S(1)} %get-tuple-element.134), channel_id=1, source_target_pairs={{0,16},{1,17},{2,18},{3,19},{4,20},{5,21},{6,22},{7,23},{8,24},{9,... | collective-permute-start | bytes 1843208 | tf_op jit(solution)/shard_map/ppermute | solution.py:682
  293.4 10.6 %collective-permute-start.24 = (bf16[2,24,3072]{2,1,0:T(8,128)(2,1)S(1)}, bf16[2,24,3072]{2,1,0:T(8,128)(2,1)S(1)}, u32[]{:S(2)}, u32[]{:S(2)}) collective-permute-start(bf16[2,24,3072]{2,1,0:T(8,128)(2,1)S(1)} %get-tuple-element.146), channel_id=1, source_target_pairs={{0,1},{1,0},{2,3},{3,2},{4,5},{5,4},{6,7},{7,6},{8,9},{9,8},{10,11... | collective-permute-start | bytes 884744 | tf_op jit(solution)/shard_map/ppermute | solution.py:682
  297.2 17.9 %collective-permute-start.29 = (bf16[2,96,768]{2,1,0:T(8,128)(2,1)S(1)}, bf16[2,96,768]{2,1,0:T(8,128)(2,1)S(1)}, u32[]{:S(2)}, u32[]{:S(2)}) collective-permute-start(bf16[2,96,768]{2,1,0:T(8,128)(2,1)S(1)} %get-tuple-element.144), channel_id=1, source_target_pairs={{0,1},{1,0},{2,3},{3,2},{4,5},{5,4},{6,7},{7,6},{8,9},{9,8},{10,11... | collective-permute-start | bytes 884744 | tf_op jit(solution)/shard_map/ppermute | solution.py:682
  304.1 11.5 %collective-permute-start.25 = (bf16[24,3072]{1,0:T(8,128)(2,1)S(1)}, bf16[24,3072]{1,0:T(8,128)(2,1)S(1)}, u32[]{:S(2)}, u32[]{:S(2)}) collective-permute-start(bf16[24,3072]{1,0:T(8,128)(2,1)S(1)} %fusion.16), channel_id=1, source_target_pairs={{0,2},{1,3},{2,0},{3,1},{4,6},{5,7},{6,4},{7,5},{8,10},{9,11},{10,... | collective-permute-start | bytes 442376 | tf_op jit(solution)/shard_map/ppermute | solution.py:682
  307.1 13.3 %collective-permute-start.19 = (bf16[2,24,3200]{2,1,0:T(8,128)(2,1)S(1)}, bf16[2,24,3200]{2,1,0:T(8,128)(2,1)S(1)}, u32[]{:S(2)}, u32[]{:S(2)}) collective-permute-start(bf16[2,24,3200]{2,1,0:T(8,128)(2,1)S(1)} %get-tuple-element.142), channel_id=1, source_target_pairs={{0,1},{1,0},{2,3},{3,2},{4,5},{5,4},{6,7},{7,6},{8,9},{9,8},{10,11... | collective-permute-start | bytes 921608 | tf_op jit(solution)/shard_map/ppermute | solution.py:682
  315.1 12.5 %collective-permute-start.30 = (bf16[96,768]{1,0:T(8,128)(2,1)S(1)}, bf16[96,768]{1,0:T(8,128)(2,1)S(1)}, u32[]{:S(2)}, u32[]{:S(2)}) collective-permute-start(bf16[96,768]{1,0:T(8,128)(2,1)S(1)} %fusion.18), channel_id=1, source_target_pairs={{0,2},{1,3},{2,0},{3,1},{4,6},{5,7},{6,4},{7,5},{8,10},{9,11},{10,... | collective-permute-start | bytes 442376 | tf_op jit(solution)/shard_map/ppermute | solution.py:682
  320.5 10.1 %collective-permute-start.20 = (bf16[24,3200]{1,0:T(8,128)(2,1)S(1)}, bf16[24,3200]{1,0:T(8,128)(2,1)S(1)}, u32[]{:S(2)}, u32[]{:S(2)}) collective-permute-start(bf16[24,3200]{1,0:T(8,128)(2,1)S(1)} %fusion.14), channel_id=1, source_target_pairs={{0,2},{1,3},{2,0},{3,1},{4,6},{5,7},{6,4},{7,5},{8,10},{9,11},{10,... | collective-permute-start | bytes 460808 | tf_op jit(solution)/shard_map/ppermute | solution.py:682
  (16 other events, 56.0 us)
